TPU v7x, 256 devices: a whole 4x4x8 slice. The times are simulated.
256 devices in a mesh: blk: 64 (over z_hi, y, x), dom: 4 (over z_lo, core).
Axes of the slice: x: 4, y: 4, z: 8 (z_hi: 4, z_lo: 2; z = z_hi * 2 + z_lo), core: 2. Of those that a mesh axis runs over, the one named last changes fastest.
Arguments:
- pno_basis: float32 [2048, 64, 256], P(('blk', 'dom')), may hold values from -0.375 to 0.375
- amplitudes: float32 [2048, 4096], P(('blk', 'dom')), may hold values from -6 to 6
- send_list: int32 [64, 4, 64, 1], P('blk', 'dom'), may hold values from 0 to 7
- couple: int32 [2048, 8], P(('blk', 'dom')), may hold values from 0 to 63, as said below
- couple_weight: float32 [2048, 8], P(('blk', 'dom')), may hold values from 0.25 to 1
- fit_weight: float32 [2048, 16], P(('blk', 'dom')), may hold values from 0.25 to 1
- fit_blocks: float32 [128, 2, 256, 256], P('blk', None, 'dom'), may hold values from -0.375 to 0.375
Outputs:
- updated: float32 [2048, 4096], P(('blk', 'dom'))
Inputs may be any that keep to these rules, and one draw needn't show every extreme that they name: `couple`: slot j of a device holds what peer j // 1 of blk sent it in its place j % 1; on every device each slot is named by at least one coupling.
All inputs are finite; a program needn't handle non-finite values.
Results may differ from a plain program's by a relative error of at most 0.0003.
Values sent between devices are 32-bit elements; how exact they have to be, the bound alone decides.
A program may use at most 64 MiB of HBM per device.

v0:
```python
import jax
import jax.numpy as jnp
from jax import lax
from jax.sharding import PartitionSpec as P

STOPS = 8


HIGHEST = lax.Precision.HIGHEST


def from_behind(x, axis, by):
    count = lax.axis_size(axis)
    return lax.ppermute(x, axis, [(i, (i + by) % count) for i in range(count)])


def dress_with(pair_amps, intersection, partner_amps, weights):
    half_product = jnp.einsum("pcab,pcbe->pcae", intersection, partner_amps, precision=HIGHEST)
    sandwich = jnp.einsum("pcae,pcfe->pcaf", half_product, intersection, precision=HIGHEST)
    return pair_amps + jnp.einsum("pc,pcaf->paf", weights, sandwich, precision=HIGHEST)


def fit_term(pair_basis, dressed, blocks, weights):
    pair_count, pno_count, orbital_count = pair_basis.shape
    flat_basis = pair_basis.reshape(pair_count * pno_count, orbital_count)
    stacked = blocks.reshape(2 * orbital_count, orbital_count)
    projected = jnp.dot(
        flat_basis, stacked.T, precision=HIGHEST, preferred_element_type=jnp.float32
    )
    projected = projected.reshape(pair_count, pno_count, 2, orbital_count)
    inner_blocks = jnp.einsum("par,pbmr->mpab", pair_basis, projected, precision=HIGHEST)
    left_product = jnp.einsum("pai,pij->paj", inner_blocks[0], dressed, precision=HIGHEST)
    fit_contrib = jnp.einsum("paj,pbj->pab", left_product, inner_blocks[1], precision=HIGHEST)
    return weights[:, None, None] * fit_contrib


def add_stop(updated_amps, pair_basis, dressed, whole_blocks, fit_weight, stop_index):
    block_total = whole_blocks.shape[0]
    for block_index in range(block_total):
        updated_amps = updated_amps + fit_term(
            pair_basis,
            dressed,
            whole_blocks[block_index],
            fit_weight[:, stop_index * block_total + block_index],
        )
    return updated_amps


def on_device(pno_basis, amplitudes, send_list, couple, couple_weight, fit_weight, fit_blocks):
    pair_count, pno_count, orbital_count = pno_basis.shape
    pair_amps = amplitudes.reshape(pair_count, pno_count, pno_count)
    send_order = send_list.reshape(-1)
    basis_out = jnp.take(pno_basis, send_order, axis=0)
    amps_out = jnp.take(amplitudes, send_order, axis=0)
    couple_count = couple.shape[1]
    basis_in, amps_in = (
        lax.all_to_all(basis_out, "blk", split_axis=0, concat_axis=0, tiled=True),
        lax.all_to_all(amps_out, "blk", split_axis=0, concat_axis=0, tiled=True),
    )
    partner_basis = jnp.take(basis_in, couple, axis=0)
    intersection = jnp.einsum("par,pcbr->pcab", pno_basis, partner_basis, precision=HIGHEST)
    partner_amps = jnp.take(amps_in, couple, axis=0).reshape(
        pair_count, couple_count, pno_count, pno_count
    )
    dressed = dress_with(pair_amps, intersection, partner_amps, couple_weight)
    updated_amps = dressed
    current = lax.all_gather(fit_blocks, "dom", axis=2, tiled=True)
    for stop_index in range(STOPS):
        if stop_index > 0:
            current = from_behind(current, "blk", 1)
        updated_amps = add_stop(updated_amps, pno_basis, dressed, current, fit_weight, stop_index)
    return updated_amps.reshape(pair_count, pno_count * pno_count)


def solution(mesh):
    placed = (
        P(("blk", "dom"), None, None),
        P(("blk", "dom"), None),
        P("blk", "dom", None, None),
        P(("blk", "dom"), None),
        P(("blk", "dom"), None),
        P(("blk", "dom"), None),
        P("blk", None, "dom", None),
    )
    return jax.shard_map(
        on_device, mesh=mesh, in_specs=placed, out_specs=P(("blk", "dom"), None), check_vma=False
    )
```

profile of v0, /device:TPU:32, one launch (start us, length us, event | category | flops | bytes accessed | tf_op | source)
XLA Modules:
  0.0 506.8 jit_solution(14811800605391812003)
XLA Ops:
  7.9 2.3 gather_fusion.2
  10.4 2.1 copy.24
  12.4 13.7 %all-to-all-start.1 = ((f32[64,1,4096]{2,1,0:T(1,128)}), f32[64,1,4096]{2,1,0:T(1,128)S(1)}, u32[]{:S(2)}, u32[]{:S(2)}) async-start(f32[64,1,4096]{2,1,0:T(1,128)} %copy.24), calls=%async_computation.1 | async-start | bytes 2097152 | tf_op jit(solution)/shard_map/all_to_all | solution.py:58
  26.9 2.8 gather_fusion
  29.7 4.5 broadcast_select_fusion
  34.2 25.5 %all-to-all-done.1 = f32[64,1,4096]{2,1,0:T(1,128)S(1)} async-done(((f32[64,1,4096]{2,1,0:T(1,128)}), f32[64,1,4096]{2,1,0:T(1,128)S(1)}, u32[]{:S(2)}, u32[]{:S(2)}) %all-to-all-start.1) | async-done | bytes 1048608 | tf_op jit(solution)/shard_map/all_to_all | solution.py:58
  59.7 6.0 %all-to-all-start = ((f32[64,64,256]{2,1,0:T(8,128)}), f32[64,64,256]{2,1,0:T(8,128)}, u32[]{:S(2)}, u32[]{:S(2)}) async-start(f32[64,64,256]{2,1,0:T(8,128)} %broadcast_select_fusion), calls=%async_computation | async-start | bytes 8388608 | tf_op jit(solution)/shard_map/all_to_all | solution.py:57
  66.4 2.1 collective-permute-start
  68.5 2.1 fusion.41
  70.6 1.8 convolution_bitcast_fusion.15
  73.5 1.0 convolution_bitcast_fusion.14
  75.2 1.9 gather_fusion.3
  77.0 2.0 gather.25
  79.1 127.5 %collective-permute-done = f32[2,2,256,256]{3,2,1,0:T(8,128)} collective-permute-done((f32[2,2,256,256]{3,2,1,0:T(8,128)}, f32[2,2,256,256]{3,2,1,0:T(8,128)}, u32[]{:S(2)}, u32[]{:S(2)}) %collective-permute-start) | collective-permute-done | bytes 1048608 | tf_op jit(solution)/shard_map/ppermute | solution.py:14
  206.5 2.1 fusion.39
  208.7 1.9 convolution_bitcast_fusion.13
  210.5 2.1 fusion.38
  212.6 1.9 convolution_bitcast_fusion.12
  214.5 37.5 %collective-permute-done.1 = f32[2,2,256,256]{3,2,1,0:T(8,128)S(1)} collective-permute-done((f32[2,2,256,256]{3,2,1,0:T(8,128)}, f32[2,2,256,256]{3,2,1,0:T(8,128)S(1)}, u32[]{:S(2)}, u32[]{:S(2)}) %collective-permute-start.1) | collective-permute-done | bytes 1048608 | tf_op jit(solution)/shard_map/ppermute | solution.py:14
  253.2 1.9 convolution_bitcast_fusion.11
  256.1 1.9 convolution_bitcast_fusion.10
  258.0 39.9 %collective-permute-done.2 = f32[2,2,256,256]{3,2,1,0:T(8,128)S(1)} collective-permute-done((f32[2,2,256,256]{3,2,1,0:T(8,128)S(1)}, f32[2,2,256,256]{3,2,1,0:T(8,128)S(1)}, u32[]{:S(2)}, u32[]{:S(2)}) %collective-permute-start.2) | collective-permute-done | bytes 1048608 | tf_op jit(solution)/shard_map/ppermute | solution.py:14
  297.9 1.0 fusion.35
  298.9 1.9 convolution_bitcast_fusion.9
  301.9 1.8 convolution_bitcast_fusion.8
  303.7 38.8 %collective-permute-done.3 = f32[2,2,256,256]{3,2,1,0:T(8,128)S(1)} collective-permute-done((f32[2,2,256,256]{3,2,1,0:T(8,128)S(1)}, f32[2,2,256,256]{3,2,1,0:T(8,128)S(1)}, u32[]{:S(2)}, u32[]{:S(2)}) %collective-permute-start.3) | collective-permute-done | bytes 1048608 | tf_op jit(solution)/shard_map/ppermute | solution.py:14
  342.9 1.0 fusion.33
  343.9 1.8 convolution_bitcast_fusion.7
  346.8 1.9 convolution_bitcast_fusion.6
  348.6 40.7 %collective-permute-done.4 = f32[2,2,256,256]{3,2,1,0:T(8,128)S(1)} collective-permute-done((f32[2,2,256,256]{3,2,1,0:T(8,128)S(1)}, f32[2,2,256,256]{3,2,1,0:T(8,128)S(1)}, u32[]{:S(2)}, u32[]{:S(2)}) %collective-permute-start.4) | collective-permute-done | bytes 1048608 | tf_op jit(solution)/shard_map/ppermute | solution.py:14
  389.4 1.0 fusion.31
  390.4 1.9 convolution_bitcast_fusion.5
  393.3 1.8 convolution_bitcast_fusion.4
  395.2 27.0 %collective-permute-done.5 = f32[2,2,256,256]{3,2,1,0:T(8,128)} collective-permute-done((f32[2,2,256,256]{3,2,1,0:T(8,128)S(1)}, f32[2,2,256,256]{3,2,1,0:T(8,128)}, u32[]{:S(2)}, u32[]{:S(2)}) %collective-permute-start.5) | collective-permute-done | bytes 1048608 | tf_op jit(solution)/shard_map/ppermute | solution.py:14
  422.2 2.1 fusion.29
  424.3 1.8 convolution_bitcast_fusion.3
  426.1 2.1 fusion.28
  428.2 1.8 convolution_bitcast_fusion.2
  430.0 5.0 gather_fusion.1
  435.0 5.8 %fusion = f32[8,8,64,64]{3,2,1,0:T(8,128)S(1)} fusion(f32[8,8,64,256]{3,2,1,0:T(8,128)} %bitcast.331, pred[8,8]{1,0:T(8,128)(4,1)S(1)} %compare_and_fusion, f32[8,64,256]{2,1,0:T(8,128)S(1)} %copy-done), kind=kOutput, calls=%fused_computation.4 | convolution fusion | flops 806354944 | bytes 5767232 | tf_op jit(solution)/shard_map/par,pcbr->pcab/dot_general | solution.py:61
  440.8 3.6 fusion.4
  444.4 2.3 fusion.94
  446.7 3.1 fusion.2
  464.3 26.1 %collective-permute-done.6 = f32[2,2,256,256]{3,2,1,0:T(8,128)} collective-permute-done((f32[2,2,256,256]{3,2,1,0:T(8,128)}, f32[2,2,256,256]{3,2,1,0:T(8,128)}, u32[]{:S(2)}, u32[]{:S(2)}) %collective-permute-start.6) | collective-permute-done | bytes 1048608 | tf_op jit(solution)/shard_map/ppermute | solution.py:14
  490.4 2.1 fusion.27
  492.5 1.3 convolution_bitcast_fusion.1
  494.4 2.1 fusion.26
  496.4 1.0 convolution_bitcast_fusion
  (99 shorter events, 27.1 us)
Async XLA Ops:
  6.5 20.3 %copy-start = (f32[8,64,256]{2,1,0:T(8,128)S(1)}, f32[8,64,256]{2,1,0:T(8,128)}, u32[]{:S(2)}) copy-start(f32[8,64,256]{2,1,0:T(8,128)} %param.7) | copy-start | bytes 1572868
  12.4 47.2 %all-to-all-start.1 = ((f32[64,1,4096]{2,1,0:T(1,128)}), f32[64,1,4096]{2,1,0:T(1,128)S(1)}, u32[]{:S(2)}, u32[]{:S(2)}) async-start(f32[64,1,4096]{2,1,0:T(1,128)} %copy.24), calls=%async_computation.1 | async-start | bytes 2097152 | tf_op jit(solution)/shard_map/all_to_all | solution.py:58
  26.1 40.3 %all-gather.2.cloned.1.call-start = ((), (), s32[]{:S(2)}) async-start(), calls=%async_computation.2 | async-start | bytes 1310720 | tf_op jit(solution)/shard_map/all_gather | solution.py:67
  34.1 31.6 %copy-start.17 = (s32[8,8]{1,0:T(8,128)S(1)}, s32[8,8]{1,0:T(8,128)}, u32[]{:S(2)}) copy-start(s32[8,8]{1,0:T(8,128)} %param.10) | copy-start | bytes 772
  34.2 31.6 %copy-start.1 = (f32[8,4096]{1,0:T(8,128)S(1)}, f32[8,4096]{1,0:T(8,128)}, u32[]{:S(2)}) copy-start(f32[8,4096]{1,0:T(8,128)} %param.8) | copy-start | bytes 393220
  34.2 31.8 %copy-start.15 = (f32[8,16]{1,0:T(8,128)S(1)}, f32[8,16]{1,0:T(8,128)}, u32[]{:S(2)}) copy-start(f32[8,16]{1,0:T(8,128)} %param.12) | copy-start | bytes 1540
  59.7 370.4 %all-to-all-start = ((f32[64,64,256]{2,1,0:T(8,128)}), f32[64,64,256]{2,1,0:T(8,128)}, u32[]{:S(2)}, u32[]{:S(2)}) async-start(f32[64,64,256]{2,1,0:T(8,128)} %broadcast_select_fusion), calls=%async_computation | async-start | bytes 8388608 | tf_op jit(solution)/shard_map/all_to_all | solution.py:57
  66.4 6.1 %copy-start.16 = (f32[2,2,256,256]{3,2,1,0:T(8,128)S(1)}, f32[2,2,256,256]{3,2,1,0:T(8,128)}, u32[]{:S(2)}) copy-start(f32[2,2,256,256]{3,2,1,0:T(8,128)} %all-gather.2.cloned.1.call-done) | copy-start | bytes 3145732
  66.4 140.1 %collective-permute-start = (f32[2,2,256,256]{3,2,1,0:T(8,128)}, f32[2,2,256,256]{3,2,1,0:T(8,128)}, u32[]{:S(2)}, u32[]{:S(2)}) collective-permute-start(f32[2,2,256,256]{3,2,1,0:T(8,128)} %all-gather.2.cloned.1.call-done), channel_id=1, source_target_pairs={{0,4},{4,8},{8,12},{12,16},{16,20},{20,24},{24,28},{28,32},{32,36}... | collective-permute-start | bytes 3145736 | tf_op jit(solution)/shard_map/ppermute | solution.py:14
  206.5 45.5 %collective-permute-start.1 = (f32[2,2,256,256]{3,2,1,0:T(8,128)}, f32[2,2,256,256]{3,2,1,0:T(8,128)S(1)}, u32[]{:S(2)}, u32[]{:S(2)}) collective-permute-start(f32[2,2,256,256]{3,2,1,0:T(8,128)} %collective-permute-done), channel_id=1, source_target_pairs={{0,4},{4,8},{8,12},{12,16},{16,20},{20,24},{24,28},{28,32},{32,36}... | collective-permute-start | bytes 3145736 | tf_op jit(solution)/shard_map/ppermute | solution.py:14
  252.0 45.9 %collective-permute-start.2 = (f32[2,2,256,256]{3,2,1,0:T(8,128)S(1)}, f32[2,2,256,256]{3,2,1,0:T(8,128)S(1)}, u32[]{:S(2)}, u32[]{:S(2)}) collective-permute-start(f32[2,2,256,256]{3,2,1,0:T(8,128)S(1)} %collective-permute-done.1), channel_id=1, source_target_pairs={{0,4},{4,8},{8,12},{12,16},{16,20},{20,24},{24,28},{28,32},{32,36}... | collective-permute-start | bytes 3145736 | tf_op jit(solution)/shard_map/ppermute | solution.py:14
  297.9 44.6 %collective-permute-start.3 = (f32[2,2,256,256]{3,2,1,0:T(8,128)S(1)}, f32[2,2,256,256]{3,2,1,0:T(8,128)S(1)}, u32[]{:S(2)}, u32[]{:S(2)}) collective-permute-start(f32[2,2,256,256]{3,2,1,0:T(8,128)S(1)} %collective-permute-done.2), channel_id=1, source_target_pairs={{0,4},{4,8},{8,12},{12,16},{16,20},{20,24},{24,28},{28,32},{32,36}... | collective-permute-start | bytes 3145736 | tf_op jit(solution)/shard_map/ppermute | solution.py:14
  342.5 46.9 %collective-permute-start.4 = (f32[2,2,256,256]{3,2,1,0:T(8,128)S(1)}, f32[2,2,256,256]{3,2,1,0:T(8,128)S(1)}, u32[]{:S(2)}, u32[]{:S(2)}) collective-permute-start(f32[2,2,256,256]{3,2,1,0:T(8,128)S(1)} %collective-permute-done.3), channel_id=1, source_target_pairs={{0,4},{4,8},{8,12},{12,16},{16,20},{20,24},{24,28},{28,32},{32,36}... | collective-permute-start | bytes 3145736 | tf_op jit(solution)/shard_map/ppermute | solution.py:14
  389.4 32.8 %collective-permute-start.5 = (f32[2,2,256,256]{3,2,1,0:T(8,128)S(1)}, f32[2,2,256,256]{3,2,1,0:T(8,128)}, u32[]{:S(2)}, u32[]{:S(2)}) collective-permute-start(f32[2,2,256,256]{3,2,1,0:T(8,128)S(1)} %collective-permute-done.4), channel_id=1, source_target_pairs={{0,4},{4,8},{8,12},{12,16},{16,20},{20,24},{24,28},{28,32},{32,36}... | collective-permute-start | bytes 3145736 | tf_op jit(solution)/shard_map/ppermute | solution.py:14
  422.2 68.2 %collective-permute-start.6 = (f32[2,2,256,256]{3,2,1,0:T(8,128)}, f32[2,2,256,256]{3,2,1,0:T(8,128)}, u32[]{:S(2)}, u32[]{:S(2)}) collective-permute-start(f32[2,2,256,256]{3,2,1,0:T(8,128)} %collective-permute-done.5), channel_id=1, source_target_pairs={{0,4},{4,8},{8,12},{12,16},{16,20},{20,24},{24,28},{28,32},{32,36}... | collective-permute-start | bytes 3145736 | tf_op jit(solution)/shard_map/ppermute | solution.py:14
  444.4 2.3 copy-start.18
  446.7 3.2 copy-start.2
  446.7 4.4 copy-start.4
  449.8 1.9 copy-start.3
  449.8 2.5 copy-start.6
  449.9 3.3 copy-start.5
  450.5 3.3 copy-start.8
  451.1 3.3 copy-start.7
  451.8 3.3 copy-start.10
  452.4 3.3 copy-start.9
  453.2 3.1 copy-start.12
  453.8 3.0 copy-start.11
  454.5 3.0 copy-start.14
  460.5 1.6 copy-start.13
Sparse Core Ops, SparseCore 0:
  28.7 29.0 all-gather.1
where the time goes:
time: 515 us; the launch traced here: 507 us
  waiting for transfers between devices  364 us (71%)
  matrix products  82.1 us (16%)
  starting transfers between devices  22.4 us (4%)
  local copies, waits for them, and re-layouts  18 us (3%)
  between operations  14.4 us (3%)
  other arithmetic  6.09 us (1%)
    ppermute x7, waiting for transfers between devices, from_behind(): return lax.ppermute(x, axis, [(i, (i + by) % count) for i in range(count)])  338 us
    dot_general x16, matrix products, fit_term(): jnp.einsum('par,pbmr->mpab', pair_basis, projected, precision=HIGHEST)  27.5 us
    all_to_all x1, waiting for transfers between devices, on_device(): lax.all_to_all(amps_out, 'blk', split_axis=0, concat_axis=0, tiled=True)  25.5 us
    dot_general x16, matrix products, fit_term(): jnp.dot(flat_basis, stacked.T, precision=HIGHEST, preferred_element_type=...  23.9 us
    all_to_all x1, starting transfers between devices, on_device(): lax.all_to_all(amps_out, 'blk', split_axis=0, concat_axis=0, tiled=True)  13.7 us
  transfers between devices with their start and end apart: 10, of which 8 were waited for; matrix products, arithmetic and copies ran while one was open for 18% of the time, Pallas kernels for 0%

commit v1 on v0

v1 whole, which is shorter than its diff:
```python
import functools

import jax
import jax.numpy as jnp
from jax import lax
from jax.experimental import pallas as pl
from jax.experimental.pallas import tpu as pltpu
from jax.sharding import PartitionSpec as P

MESH = pl.DeviceIdType.MESH
BF, F32 = jnp.bfloat16, jnp.float32
PAIRS, PNO, ORB = 8, 64, 256
ROWS = PNO + 16
SLOTS = 64

SHARD, BASES, WEIGHTS, TABLE, Z1A, Z1B, Z3A, Z3B, RELAYA, RELAYB, FY, FX, CORE, DSEND, PSEND = (
    0, 1, 2, 2, 6, 7, 8, 9, 10, 11, 12, 12, 16, 20, 21,
)
TRANSFERS = 22
NN = (((1,), (0,)), ((), ()))
NT = (((1,), (1,)), ((), ()))


def split(v):
    high = v.astype(BF)
    return high, (v - high.astype(F32)).astype(BF)


def dot3(a, b, dims):
    one = functools.partial(lax.dot_general, dimension_numbers=dims, preferred_element_type=F32)
    return one(a[0], b[0]) + (one(a[0], b[1]) + one(a[1], b[0]))


def natural(a4):
    return jnp.concatenate([a4[:, PNO * u : PNO * (u + 1)] for u in range(4)], axis=0)


def place():
    blk, dom = lax.axis_index("blk"), lax.axis_index("dom")
    return lax.div(blk, 16), lax.rem(lax.div(blk, 4), 4), lax.rem(blk, 4), lax.div(dom, 2), lax.rem(dom, 2)


def device(zh, y, x, zl, core):
    return (lax.rem(zh, 4) * 4 + lax.rem(y, 4)) * 4 + lax.rem(x, 4), zl * 2 + core


def kernel(
    sends_ref, readers_ref, where_ref, scale_ref,
    packed, shard, weights, tables,
    out_ref,
    z1, z2, z3, tables_in, tables_sm, stage, arrived, whole, slots, partner_bases, partner_weights,
    basis_h, basis_l, other_h, other_l, block_h, block_l, proj_h, proj_l,
    f0_h, f0_l, f1_h, f1_l, terms, dressed, d_send, d_recv, part_send, part_recv,
    plane_send, plane_recv, send_sem, recv_sem, local_sem,
):
    zh, y, x, zl, core = place()
    partner = device(zh, y, x, 1 - zl, core)
    twin = device(zh, y, x, zl, 1 - core)
    up, down, across = (device(zh + k, y, x, zl, core) for k in (1, 3, 2))
    step_y = 2 - zl
    fit_to = device(zh + lax.div(y + step_y, 4), y + step_y, x, zl, core)
    fit_from = device(zh + 3 + lax.div(y + 4 - step_y, 4), y + 4 - step_y, x, zl, core)

    def across_plane(t):
        return device(zh, y + lax.div(t, 4), x + lax.rem(t, 4), zl, core)

    def copy(n, src, dst, to):
        return pltpu.make_async_remote_copy(
            src_ref=src, dst_ref=dst, send_sem=send_sem.at[n], recv_sem=recv_sem.at[n],
            device_id=to, device_id_type=MESH,
        )

    def plane_copy(dz, t):
        n = dz * 16 + t
        return pltpu.make_async_remote_copy(
            src_ref=stage.at[n], dst_ref=arrived.at[n], send_sem=plane_send.at[n], recv_sem=plane_recv.at[n],
            device_id=across_plane(t), device_id_type=MESH,
        )

    sh = copy(SHARD, shard, whole.at[0, zl], partner)
    bases = copy(BASES, packed.at[:, pl.ds(0, PNO), :], partner_bases, partner)
    wts = copy(WEIGHTS, weights.at[1], partner_weights, partner)
    tabs = {dz: copy(TABLE + dz, tables.at[dz], tables_in.at[dz], to) for dz, to in ((1, up), (2, across), (3, down))}
    low, high = pl.ds(0, 4), pl.ds(4, 4)
    z1a = copy(Z1A, packed.at[low], z1.at[low], up)
    z1b = copy(Z1B, packed.at[high], z1.at[high], up)
    z3a = copy(Z3A, packed.at[low], z3.at[low], down)
    z3b = copy(Z3B, packed.at[high], z3.at[high], down)
    relay_a = copy(RELAYA, z1.at[low], z2.at[low], up)
    relay_b = copy(RELAYB, z3.at[high], z2.at[high], down)
    fy = copy(FY, whole.at[0], whole.at[1], fit_to)

    def fx(dx, which):
        return copy(FX + dx, whole.at[which], slots.at[dx, :, core], device(zh, y, x + dx, zl, core))

    def to_twin(j):
        return copy(CORE + j, slots.at[j, :, core], slots.at[j, :, core], twin)

    def first_slot(which):
        pltpu.make_async_copy(whole.at[which], slots.at[0, :, core], local_sem.at[1]).start()
        copy(CORE, whole.at[which], slots.at[0, :, core], twin).start()

    def fill_stage(source, index_of, dz):
        arrived[dz * 16] = source[index_of(0)]

        def one(t, _):
            stage[dz * 16 + t] = source[index_of(t)]
            return 0

        lax.fori_loop(1, 16, one, 0)

    def send_stage(dz):
        def one(t, _):
            plane_copy(dz, t).start()
            return 0

        lax.fori_loop(1, 16, one, 0)

    barrier = pltpu.get_barrier_semaphore()

    def greet(to):
        pl.semaphore_signal(barrier, inc=1, device_id=to, device_id_type=MESH)

    def greet_plane(t, _):
        greet(across_plane(t))
        return 0

    lax.fori_loop(1, 16, greet_plane, 0)
    for to in (partner, twin, up, down, across, fit_to, fit_from):
        greet(to)
    own_shard = pltpu.make_async_copy(shard, whole.at[0, zl], local_sem.at[0])
    own_shard.start()
    fill_stage(packed, lambda t: sends_ref[t], 0)

    def split_own(p, _):
        basis_h[p], basis_l[p] = split(packed[p, :PNO, :])
        return 0

    lax.fori_loop(0, PAIRS, split_own, 0)
    own_shard.wait()
    pl.semaphore_wait(barrier, 22)

    sh.start()
    for dz in (1, 3, 2):
        tabs[dz].start()
    z1a.start()
    z3b.start()
    send_stage(0)
    z1b.start()
    z3a.start()
    wts.start()
    bases.start()

    sh.wait_recv()
    fy.start()

    @pl.when(zl == 0)
    def _():
        first_slot(0)

    def own_rows(dx):
        return (1 - zl) * (1 - lax.div(x + dx, 4))

    for dx in (1, 3, 2):

        @pl.when(own_rows(dx) == 1)
        def _():
            fx(dx, 0).start()

    z1a.wait_recv()
    relay_a.start()
    z3b.wait_recv()
    relay_b.start()
    fy.wait_recv()
    for dx in (1, 3, 2):

        @pl.when(own_rows(dx) == 0)
        def _():
            fx(dx, 1).start()

    @pl.when(zl == 1)
    def _():
        first_slot(1)

    def pass_on(dz, source):
        tabs[dz].wait_recv()
        table = pltpu.make_async_copy(tables_in.at[dz], tables_sm.at[dz], local_sem.at[1 + dz])
        table.start()
        table.wait()
        fill_stage(source, lambda t: tables_sm[dz, 0, t], dz)
        send_stage(dz)

    def dress(dz):
        def one_of(t):
            return pltpu.make_async_remote_copy(
                src_ref=stage.at[t], dst_ref=arrived.at[t], send_sem=plane_send.at[t], recv_sem=plane_recv.at[t],
                device_id=twin, device_id_type=MESH,
            )

        def arrive(t, _):
            one_of(t).wait_recv()
            return 0

        lax.fori_loop(dz * 16 + 1, dz * 16 + 16, arrive, 0)

        def some(i, _):
            for u in range(4):
                t = dz * 16 + i * 4 + u
                reader = readers_ref[t]
                own = basis_h[reader], basis_l[reader]
                overlap = split(dot3(own, split(arrived[t, :PNO, :]), NT))
                half = split(dot3(overlap, split(natural(arrived[t, PNO:, :])), NN))
                terms[t] = scale_ref[t] * dot3(half, overlap, NT)
            return 0

        lax.fori_loop(0, 4, some, 0)

    def fit(j, group):
        bases_h, bases_l = (basis_h, basis_l) if group == 0 else (other_h, other_l)
        rows_of = weights.at[0] if group == 0 else partner_weights

        def project(n, _):
            flat = (bases_h[...].reshape(PAIRS * PNO, ORB), bases_l[...].reshape(PAIRS * PNO, ORB))
            proj_h[n], proj_l[n] = split(dot3(flat, (block_h[n], block_l[n]), NN))
            return 0

        lax.fori_loop(0, 4, project, 0)

        def pair(p, _):
            rows = pl.ds(pl.multiple_of(p * PNO, PNO), PNO)
            left = proj_h[:, rows, :].reshape(4 * PNO, ORB), proj_l[:, rows, :].reshape(4 * PNO, ORB)
            both = dot3(left, (bases_h[p], bases_l[p]), NT)
            n = group * PAIRS + p
            for k in range(2):
                weight = rows_of[pl.ds(p * 8 + j * 2 + k, 1), :][:, :PNO]
                to = pl.ds((j * 2 + k) * PNO, PNO)
                f0_h[n, to, :], f0_l[n, to, :] = split(both[k * PNO : (k + 1) * PNO] * weight)
                f1_h[n, to, :], f1_l[n, to, :] = split(both[(2 + k) * PNO : (3 + k) * PNO])
            return 0

        lax.fori_loop(0, PAIRS, pair, 0)

    def load_blocks(j):
        for n in range(4):
            m, k = n // 2, n % 2
            rows = [slots[j, a, b, k, m] for a in range(2) for b in range(2)]
            block_h[n], block_l[n] = split(jnp.concatenate(rows, axis=0))

    z1b.wait_recv()
    pass_on(1, z1)
    z3a.wait_recv()
    pass_on(3, z3)
    dress(0)
    to_twin(0).wait_recv()
    pltpu.make_async_copy(whole.at[0], slots.at[0, :, core], local_sem.at[1]).wait()
    load_blocks(0)
    fit(0, 0)
    relay_a.wait_recv()
    relay_b.wait_recv()
    pass_on(2, z2)
    for dx in (1, 3, 2):
        fx(dx, 0).wait_recv()
        to_twin(dx).start()
    wts.wait_recv()
    bases.wait_recv()

    def split_other(p, _):
        other_h[p], other_l[p] = split(partner_bases[p])
        return 0

    lax.fori_loop(0, PAIRS, split_other, 0)
    fit(0, 1)
    dress(1)
    dress(3)
    for j in (1, 3, 2):
        to_twin(j).wait_recv()
        load_blocks(j)
        fit(j, 0)
        fit(j, 1)
    dress(2)

    def gather_terms(p, _):
        total = natural(packed[p, PNO:, :])
        for c in range(8):
            total = total + terms[where_ref[p * 8 + c]]
        dressed[p] = total
        return 0

    lax.fori_loop(0, PAIRS, gather_terms, 0)
    for q in range(4):
        d_send[q] = jnp.concatenate([dressed[q], dressed[q + 4]], axis=1)
    ds = copy(DSEND, d_send, d_recv, partner)
    ds.start()

    def fitted_sum(n, d):
        left = dot3((f0_h[n], f0_l[n]), split(d), NN)
        left_h, left_l = split(left)
        total = jnp.zeros((PNO, PNO), F32)
        for i in range(8):
            r = slice(i * PNO, (i + 1) * PNO)
            total = total + dot3((left_h[r], left_l[r]), (f1_h[n, r, :], f1_l[n, r, :]), NT)
        return total

    def finish_own(p, _):
        dressed[p] = dressed[p] + fitted_sum(p, dressed[p])
        return 0

    lax.fori_loop(0, PAIRS, finish_own, 0)
    ds.wait_recv()

    def finish_other(q, _):
        two = d_recv[q]
        part_send[q] = jnp.concatenate(
            [fitted_sum(PAIRS + q, two[:, :PNO]), fitted_sum(PAIRS + q + 4, two[:, PNO:])], axis=1
        )
        return 0

    lax.fori_loop(0, 4, finish_other, 0)
    ps = copy(PSEND, part_send, part_recv, partner)
    ps.start()

    for done in (sh, bases, wts, z1a, z1b, z3a, z3b, relay_a, relay_b, fy, ds, *tabs.values()):
        done.wait_send()
    for dx in (1, 2, 3):
        fx(dx, 0).wait_send()
    for j in range(4):
        to_twin(j).wait_send()

    def plane_sent(n, _):
        @pl.when(lax.rem(n, 16) > 0)
        def _():
            plane_copy(lax.div(n, 16), lax.rem(n, 16)).wait_send()

        return 0

    lax.fori_loop(0, SLOTS, plane_sent, 0)
    ps.wait()
    for q in range(4):
        two = part_recv[q]
        out_ref[q] = dressed[q] + two[:, :PNO]
        out_ref[q + 4] = dressed[q + 4] + two[:, PNO:]


def on_device(pno_basis, amplitudes, send_list, couple, couple_weight, fit_weight, fit_blocks):
    zh, y, x, zl, _ = place()
    quarters = amplitudes.reshape(PAIRS, 4, 16, PNO).transpose(0, 2, 1, 3).reshape(PAIRS, 16, ORB)
    packed = jnp.concatenate([pno_basis, quarters], axis=1)

    t = jnp.arange(SLOTS, dtype=jnp.int32)
    dz, dy, dx = t // 16, (t // 4) % 4, t % 4
    source = ((zh + 4 - dz) % 4) * 16 + ((y + 4 - dy) % 4) * 4 + (x + 4 - dx) % 4
    reads = couple.reshape(1, -1) == source[:, None]
    readers = jnp.sum(jnp.where(reads, t[None, :] // 8, 0), axis=1)
    scale = jnp.sum(jnp.where(reads, couple_weight.reshape(1, -1), 0.0), axis=1)
    where = jnp.sum(jnp.where(reads, t[:, None], 0), axis=0)
    target = ((zh + dz) % 4) * 16 + ((y + dy) % 4) * 4 + (x + dx) % 4
    sends = jnp.sum(jnp.where(target[:, None] == t[None, :], send_list.reshape(1, -1), 0), axis=1)
    tables = jnp.broadcast_to(jnp.pad(sends.reshape(4, 1, 16), ((0, 0), (0, 0), (0, 112))), (4, 8, 128))

    j = jnp.arange(8, dtype=jnp.int32) // 2
    bit = jnp.arange(8, dtype=jnp.int32) % 2
    late = jnp.where(x < j, 1, 0)
    stop_even, stop_odd = j + 4 * late, j + 4 * (1 - late)
    stops = jnp.stack([jnp.where(zl == 0, stop_even, stop_odd), jnp.where(zl == 0, stop_odd, stop_even)])
    column = stops * 2 + bit
    chosen = jnp.sum(
        jnp.where(column[:, None, :, None] == jnp.arange(16)[None, None, None, :], fit_weight[None, :, None, :], 0.0), axis=3
    )
    weights = jnp.broadcast_to(chosen.reshape(2, SLOTS, 1), (2, SLOTS, 128))

    vmem, smem = pl.BlockSpec(memory_space=pltpu.VMEM), pl.BlockSpec(memory_space=pltpu.SMEM)
    tile = functools.partial(pltpu.VMEM, dtype=F32)
    narrow = functools.partial(pltpu.VMEM, dtype=BF)
    out = pl.pallas_call(
        kernel,
        out_shape=jax.ShapeDtypeStruct((PAIRS, PNO, PNO), F32),
        in_specs=[smem] * 4 + [vmem] * 4,
        out_specs=vmem,
        scratch_shapes=[
            tile((PAIRS, ROWS, ORB)), tile((PAIRS, ROWS, ORB)), tile((PAIRS, ROWS, ORB)),
            pltpu.VMEM((4, 8, 128), jnp.int32), pltpu.SMEM((4, 8, 128), jnp.int32),
            tile((SLOTS, ROWS, ORB)), tile((SLOTS, ROWS, ORB)),
            tile((2, 2, 2, 2, PNO, ORB)), tile((4, 2, 2, 2, 2, PNO, ORB)),
            tile((PAIRS, PNO, ORB)), tile((SLOTS, 128)),
            narrow((PAIRS, PNO, ORB)), narrow((PAIRS, PNO, ORB)), narrow((PAIRS, PNO, ORB)), narrow((PAIRS, PNO, ORB)),
            narrow((4, ORB, ORB)), narrow((4, ORB, ORB)),
            narrow((4, PAIRS * PNO, ORB)), narrow((4, PAIRS * PNO, ORB)),
            narrow((16, 512, PNO)), narrow((16, 512, PNO)), narrow((16, 512, PNO)), narrow((16, 512, PNO)),
            tile((SLOTS, PNO, PNO)), tile((PAIRS, PNO, PNO)),
            tile((4, PNO, 128)), tile((4, PNO, 128)), tile((4, PNO, 128)), tile((4, PNO, 128)),
            pltpu.SemaphoreType.DMA((SLOTS,)), pltpu.SemaphoreType.DMA((SLOTS,)),
            pltpu.SemaphoreType.DMA((TRANSFERS,)), pltpu.SemaphoreType.DMA((TRANSFERS,)),
            pltpu.SemaphoreType.DMA((5,)),
        ],
        compiler_params=pltpu.CompilerParams(
            collective_id=0, has_side_effects=True, vmem_limit_bytes=60 * 1024 * 1024
        ),
    )(sends[:16], readers, where, scale, packed, fit_blocks, weights, tables)
    return out.reshape(PAIRS, PNO * PNO)


def solution(mesh):
    placed = (
        P(("blk", "dom"), None, None),
        P(("blk", "dom"), None),
        P("blk", "dom", None, None),
        P(("blk", "dom"), None),
        P(("blk", "dom"), None),
        P(("blk", "dom"), None),
        P("blk", None, "dom", None),
    )
    return jax.shard_map(
        on_device, mesh=mesh, in_specs=placed, out_specs=P(("blk", "dom"), None), check_vma=False
    )
```

time: 515 us -> 218 us (0.42); the launches traced: 507 us -> 217 us
  waiting for transfers between devices: 364 us -> 0 us
  Pallas kernels: 0 us -> 207 us
  matrix products: 82.1 us -> 0 us
  starting transfers between devices: 22.4 us -> 0 us
  between operations: 14.4 us -> 0.06 us
  local copies, waits for them, and re-layouts: 18 us -> 5.88 us
    ppermute x7 -> x0, waiting for transfers between devices: 338 us -> none  [from_behind(): return lax.ppermute(x, axis, [(i, (i + by) % count) for i in range(count)])]
    pallas_call x0 -> x1, Pallas kernels: none -> 207 us  [on_device(): pl.pallas_call(kernel, out_shape=jax.ShapeDtypeStruct((PAIRS, PNO, PNO),...]
    dot_general x68 -> x0, matrix products: 82.1 us -> none  [the longest x16 27.5 us: fit_term(): jnp.einsum('par,pbmr->mpab', pair_basis, projected, precision=HIGHEST)]
    all_to_all x2 -> x0, waiting for transfers between devices: 25.5 us -> none  [the longest x1 25.5 us: on_device(): lax.all_to_all(amps_out, 'blk', split_axis=0, concat_axis=0, tiled=True)]
    all_to_all x2 -> x0, starting transfers between devices: 19.7 us -> none  [the longest x1 13.7 us: on_device(): lax.all_to_all(amps_out, 'blk', split_axis=0, concat_axis=0, tiled=True)]
    gather x5 -> x0, local copies, waits for them, and re-layouts: 13.9 us -> none  [the longest x1 4.97 us: on_device(): partner_basis = jnp.take(basis_in, couple, axis=0)]
    select_n x4 -> x3, other arithmetic: 5.36 us -> 0.04 us  [the longest x1 0.02 us: on_device(): readers = jnp.sum(jnp.where(reads, t[None, :] // 8, 0), axis=1)]
  transfers between devices with their start and end apart: 10 -> 0, of which waited for: 8 -> 0; matrix products, arithmetic and copies ran while one was open for 18% -> 0% of each run, Pallas kernels for 0% -> 0%
where the time goes in v1:
time: 218 us; the launch traced here: 217 us
  Pallas kernels  207 us (95%)
  local copies, waits for them, and re-layouts  5.88 us (3%)
  other arithmetic  4.15 us (2%)
    pallas_call x1, Pallas kernels, on_device(): pl.pallas_call(kernel, out_shape=jax.ShapeDtypeStruct((PAIRS, PNO, PNO),...  207 us

profile of v1, /device:TPU:32, one launch (start us, length us, event | category | flops | bytes accessed | tf_op | source)
XLA Modules:
  0.0 217.4 jit_solution(8566748169518083320)
XLA Ops:
  0.0 0.0 copy-start.1
  0.0 0.9 select_reduce_fusion.1
  0.9 0.0 copy-start.2
  0.9 0.8 eq.64
  1.7 0.8 broadcast_in_dim.96
  2.5 0.8 fusion.2.scale_ref
  3.2 0.7 fusion.1
  4.0 0.1 iota_compare_fusion.1
  4.1 0.0 copy-done.2
  4.1 0.1 reshape.284
  4.1 0.8 select_reduce_fusion
  4.9 0.1 broadcast_in_dim.102
  5.0 0.6 broadcast_in_dim.105.tables
  5.6 0.7 broadcast_in_dim.103.weights
  6.3 0.0 copy-done.1
  6.3 0.1 reshape.282
  6.4 0.0 copy-start
  6.4 0.1 copy.11
  6.6 0.2 reshape.283
  6.8 0.7 copy-done
  7.5 0.9 pad_maximum_fusion.packed
  8.4 207.3 %shard_map.73 = f32[8,64,64]{2,1,0:T(8,128)} custom-call(s32[16]{0:T(128)} %bitcast.8, s32[64]{0:T(128)} %get-tuple-element.6.readers_ref, s32[64]{0:T(128)} %get-tuple-element.5.where_ref, f32[64]{0:T(128)} %fusion.2.scale_ref, f32[8,80,256]{2,1,0:T(8,128)} %pad_maximum_fusion.packed, f32[2,2,64,256]{3,2,1,0:T(8,128)} %shard.1, ...), custom_call_target="tpu_custom_call" | custom-call | tf_op jit(solution)/shard_map/pallas_call | solution.py:374
  215.6 1.7 reshape.285
  (6 shorter events, 0.1 us)
Async XLA Ops:
  0.0 6.3 %copy-start.1 = (f32[8,4096]{1,0:T(8,128)S(1)}, f32[8,4096]{1,0:T(8,128)}, u32[]{:S(2)}) copy-start(f32[8,4096]{1,0:T(8,128)} %param.8) | copy-start | bytes 393220
  0.9 3.1 %copy-start.2 = (s32[64]{0:T(128)}, s32[64]{0:T(128)S(1)}, u32[]{:S(2)}) copy-start(s32[64]{0:T(128)S(1)} %select_reduce_fusion.1) | copy-start | bytes 772
  6.4 1.0 copy-start

commit v2 on v1

--- a/solution.py
+++ b/solution.py
@@ -13,10 +13,10 @@
 ROWS = PNO + 16
 SLOTS = 64
 
-SHARD, BASES, WEIGHTS, TABLE, Z1A, Z1B, Z3A, Z3B, RELAYA, RELAYB, FY, FX, CORE, DSEND, PSEND = (
-    0, 1, 2, 2, 6, 7, 8, 9, 10, 11, 12, 12, 16, 20, 21,
+SHARD, BASES, WEIGHTS, TABLE, DSEND, PSEND, FY, CORE, UP, DOWN, RELAY, FX = (
+    0, 1, 2, 2, 6, 7, 8, 16, 20, 28, 36, 40,
 )
-TRANSFERS = 22
+TRANSFERS = 56
 NN = (((1,), (0,)), ((), ()))
 NT = (((1,), (1,)), ((), ()))
 
@@ -45,10 +45,10 @@
 
 
 def kernel(
-    sends_ref, readers_ref, where_ref, scale_ref,
-    packed, shard, weights, tables,
+    sends_ref, inverse_ref, couple_ref, scale_ref, rate_ref,
+    packed, shard, weights, table,
     out_ref,
-    z1, z2, z3, tables_in, tables_sm, stage, arrived, whole, slots, partner_bases, partner_weights,
+    z1, z2, z3, tables_in, tables_sm, stage, arrived, whole, slots, partner_bases, partner_weights, partner_rates,
     basis_h, basis_l, other_h, other_l, block_h, block_l, proj_h, proj_l,
     f0_h, f0_l, f1_h, f1_l, terms, dressed, d_send, d_recv, part_send, part_recv,
     plane_send, plane_recv, send_sem, recv_sem, local_sem,
@@ -79,19 +79,37 @@
 
     sh = copy(SHARD, shard, whole.at[0, zl], partner)
     bases = copy(BASES, packed.at[:, pl.ds(0, PNO), :], partner_bases, partner)
-    wts = copy(WEIGHTS, weights.at[1], partner_weights, partner)
-    tabs = {dz: copy(TABLE + dz, tables.at[dz], tables_in.at[dz], to) for dz, to in ((1, up), (2, across), (3, down))}
-    low, high = pl.ds(0, 4), pl.ds(4, 4)
-    z1a = copy(Z1A, packed.at[low], z1.at[low], up)
-    z1b = copy(Z1B, packed.at[high], z1.at[high], up)
-    z3a = copy(Z3A, packed.at[low], z3.at[low], down)
-    z3b = copy(Z3B, packed.at[high], z3.at[high], down)
-    relay_a = copy(RELAYA, z1.at[low], z2.at[low], up)
-    relay_b = copy(RELAYB, z3.at[high], z2.at[high], down)
-    fy = copy(FY, whole.at[0], whole.at[1], fit_to)
-
-    def fx(dx, which):
-        return copy(FX + dx, whole.at[which], slots.at[dx, :, core], device(zh, y, x + dx, zl, core))
+    wts = copy(WEIGHTS, weights, partner_weights, partner)
+    tabs = {dz: copy(TABLE + dz, table, tables_in.at[dz], to) for dz, to in ((1, up), (2, across), (3, down))}
+
+    def z_up(i):
+        return copy(UP + i, packed.at[i], z1.at[i], up)
+
+    def z_down(i):
+        return copy(DOWN + i, packed.at[i], z3.at[i], down)
+
+    def relay(i):
+        if i < 4:
+            return copy(RELAY + i, z1.at[i], z2.at[i], up)
+        return copy(RELAY + i, z3.at[i], z2.at[i], down)
+
+    def fy(a):
+        return copy(FY + a, whole.at[0, a], whole.at[1, a], fit_to)
+
+
+    def fx(dx, which, i):
+        a, k = i // 2, i % 2
+        return copy(
+            FX + dx * 4 + i, whole.at[which, a, k], slots.at[dx, a, core, k], device(zh, y, x + dx, zl, core)
+        )
+
+    def send_rows(which, pieces):
+        for i in pieces:
+            for dx in (1, 3, 2):
+
+                @pl.when(own_rows(dx) == 1 - which)
+                def _():
+                    fx(dx, which, i).start()
 
     def to_twin(j):
         return copy(CORE + j, slots.at[j, :, core], slots.at[j, :, core], twin)
@@ -100,6 +118,9 @@
         pltpu.make_async_copy(whole.at[which], slots.at[0, :, core], local_sem.at[1]).start()
         copy(CORE, whole.at[which], slots.at[0, :, core], twin).start()
 
+    def reader_of(t):
+        return (zh * 4 + lax.rem(y + lax.div(t, 4), 4)) * 4 + lax.rem(x + lax.rem(t, 4), 4)
+
     def fill_stage(source, index_of, dz):
         arrived[dz * 16] = source[index_of(0)]
 
@@ -110,11 +131,8 @@
         lax.fori_loop(1, 16, one, 0)
 
     def send_stage(dz):
-        def one(t, _):
+        for t in (1, 4, 3, 12, 5, 7, 13, 15, 2, 8, 6, 9, 14, 11, 10):
             plane_copy(dz, t).start()
-            return 0
-
-        lax.fori_loop(1, 16, one, 0)
 
     barrier = pltpu.get_barrier_semaphore()
 
@@ -130,7 +148,7 @@
         greet(to)
     own_shard = pltpu.make_async_copy(shard, whole.at[0, zl], local_sem.at[0])
     own_shard.start()
-    fill_stage(packed, lambda t: sends_ref[t], 0)
+    fill_stage(packed, lambda t: sends_ref[reader_of(t)], 0)
 
     def split_own(p, _):
         basis_h[p], basis_l[p] = split(packed[p, :PNO, :])
@@ -141,18 +159,19 @@
     pl.semaphore_wait(barrier, 22)
 
     sh.start()
+    for t in (1, 4, 3, 12, 5, 7, 13, 15):
+        plane_copy(0, t).start()
+
+    sh.wait_recv()
+    fy(0).start()
+    fy(1).start()
     for dz in (1, 3, 2):
         tabs[dz].start()
-    z1a.start()
-    z3b.start()
-    send_stage(0)
-    z1b.start()
-    z3a.start()
-    wts.start()
-    bases.start()
-
-    sh.wait_recv()
-    fy.start()
+    for i in range(4):
+        z_up(i).start()
+        z_down(4 + i).start()
+    for t in (2, 8, 6, 9, 14, 11, 10):
+        plane_copy(0, t).start()
 
     @pl.when(zl == 0)
     def _():
@@ -161,22 +180,18 @@
     def own_rows(dx):
         return (1 - zl) * (1 - lax.div(x + dx, 4))
 
-    for dx in (1, 3, 2):
-
-        @pl.when(own_rows(dx) == 1)
-        def _():
-            fx(dx, 0).start()
-
-    z1a.wait_recv()
-    relay_a.start()
-    z3b.wait_recv()
-    relay_b.start()
-    fy.wait_recv()
-    for dx in (1, 3, 2):
-
-        @pl.when(own_rows(dx) == 0)
-        def _():
-            fx(dx, 1).start()
+    for i in range(4):
+        z_up(4 + i).start()
+        z_down(i).start()
+        send_rows(0, (i,))
+    fy(0).wait_recv()
+    fy(1).wait_recv()
+    for i in range(4):
+        z_up(i).wait_recv()
+        relay(i).start()
+        z_down(4 + i).wait_recv()
+        relay(4 + i).start()
+        send_rows(1, (i,))
 
     @pl.when(zl == 1)
     def _():
@@ -187,7 +202,7 @@
         table = pltpu.make_async_copy(tables_in.at[dz], tables_sm.at[dz], local_sem.at[1 + dz])
         table.start()
         table.wait()
-        fill_stage(source, lambda t: tables_sm[dz, 0, t], dz)
+        fill_stage(source, lambda t: tables_sm[dz, 0, reader_of(t)], dz)
         send_stage(dz)
 
     def dress(dz):
@@ -206,18 +221,21 @@
         def some(i, _):
             for u in range(4):
                 t = dz * 16 + i * 4 + u
-                reader = readers_ref[t]
+                term = inverse_ref[t]
+                reader, of = lax.div(term, 8), lax.rem(term, 8)
                 own = basis_h[reader], basis_l[reader]
                 overlap = split(dot3(own, split(arrived[t, :PNO, :]), NT))
                 half = split(dot3(overlap, split(natural(arrived[t, PNO:, :])), NN))
-                terms[t] = scale_ref[t] * dot3(half, overlap, NT)
+                terms[t] = scale_ref[reader, of] * dot3(half, overlap, NT)
             return 0
 
         lax.fori_loop(0, 4, some, 0)
 
     def fit(j, group):
         bases_h, bases_l = (basis_h, basis_l) if group == 0 else (other_h, other_l)
-        rows_of = weights.at[0] if group == 0 else partner_weights
+        rates = rate_ref if group == 0 else partner_rates
+        late = lax.div(3 - x + j, 4)
+        stop = j + 4 * (zl + late - 2 * zl * late)
 
         def project(n, _):
             flat = (bases_h[...].reshape(PAIRS * PNO, ORB), bases_l[...].reshape(PAIRS * PNO, ORB))
@@ -232,10 +250,10 @@
             both = dot3(left, (bases_h[p], bases_l[p]), NT)
             n = group * PAIRS + p
             for k in range(2):
-                weight = rows_of[pl.ds(p * 8 + j * 2 + k, 1), :][:, :PNO]
                 to = pl.ds((j * 2 + k) * PNO, PNO)
-                f0_h[n, to, :], f0_l[n, to, :] = split(both[k * PNO : (k + 1) * PNO] * weight)
-                f1_h[n, to, :], f1_l[n, to, :] = split(both[(2 + k) * PNO : (3 + k) * PNO])
+                f0_h[n, to, :], f0_l[n, to, :] = split(both[k * PNO : (k + 1) * PNO] * rates[p, stop * 2 + k])
+            right = jnp.concatenate([both[2 * PNO : 3 * PNO], both[3 * PNO :]], axis=1)
+            f1_h[n, :, pl.ds(j * 128, 128)], f1_l[n, :, pl.ds(j * 128, 128)] = split(right)
             return 0
 
         lax.fori_loop(0, PAIRS, pair, 0)
@@ -246,23 +264,31 @@
             rows = [slots[j, a, b, k, m] for a in range(2) for b in range(2)]
             block_h[n], block_l[n] = split(jnp.concatenate(rows, axis=0))
 
-    z1b.wait_recv()
+    for i in range(4):
+        z_up(4 + i).wait_recv()
     pass_on(1, z1)
-    z3a.wait_recv()
+    for i in range(4):
+        z_down(i).wait_recv()
     pass_on(3, z3)
+    wts.start()
+    bases.start()
     dress(0)
     to_twin(0).wait_recv()
     pltpu.make_async_copy(whole.at[0], slots.at[0, :, core], local_sem.at[1]).wait()
     load_blocks(0)
     fit(0, 0)
-    relay_a.wait_recv()
-    relay_b.wait_recv()
+    for i in range(8):
+        relay(i).wait_recv()
     pass_on(2, z2)
     for dx in (1, 3, 2):
-        fx(dx, 0).wait_recv()
+        for i in range(4):
+            fx(dx, 0, i).wait_recv()
         to_twin(dx).start()
     wts.wait_recv()
+    rates_in = pltpu.make_async_copy(partner_weights, partner_rates, local_sem.at[1])
+    rates_in.start()
     bases.wait_recv()
+    rates_in.wait()
 
     def split_other(p, _):
         other_h[p], other_l[p] = split(partner_bases[p])
@@ -282,7 +308,9 @@
     def gather_terms(p, _):
         total = natural(packed[p, PNO:, :])
         for c in range(8):
-            total = total + terms[where_ref[p * 8 + c]]
+            slot = couple_ref[p, c]
+            back = lax.rem(zh + 4 - lax.div(slot, 16), 4) * 16 + lax.rem(y + 4 - lax.rem(lax.div(slot, 4), 4), 4) * 4
+            total = total + terms[back + lax.rem(x + 4 - lax.rem(slot, 4), 4)]
         dressed[p] = total
         return 0
 
@@ -294,12 +322,11 @@
 
     def fitted_sum(n, d):
         left = dot3((f0_h[n], f0_l[n]), split(d), NN)
-        left_h, left_l = split(left)
-        total = jnp.zeros((PNO, PNO), F32)
-        for i in range(8):
-            r = slice(i * PNO, (i + 1) * PNO)
-            total = total + dot3((left_h[r], left_l[r]), (f1_h[n, r, :], f1_l[n, r, :]), NT)
-        return total
+        left = jnp.concatenate(
+            [jnp.concatenate([left[i * PNO : (i + 1) * PNO], left[(i + 1) * PNO : (i + 2) * PNO]], axis=1) for i in (0, 2, 4, 6)],
+            axis=1,
+        )
+        return dot3(split(left), (f1_h[n], f1_l[n]), NT)
 
     def finish_own(p, _):
         dressed[p] = dressed[p] + fitted_sum(p, dressed[p])
@@ -319,10 +346,15 @@
     ps = copy(PSEND, part_send, part_recv, partner)
     ps.start()
 
-    for done in (sh, bases, wts, z1a, z1b, z3a, z3b, relay_a, relay_b, fy, ds, *tabs.values()):
+    for done in (sh, bases, wts, fy(0), fy(1), ds, *tabs.values()):
         done.wait_send()
+    for i in range(8):
+        z_up(i).wait_send()
+        z_down(i).wait_send()
+        relay(i).wait_send()
     for dx in (1, 2, 3):
-        fx(dx, 0).wait_send()
+        for i in range(4):
+            fx(dx, 0, i).wait_send()
     for j in range(4):
         to_twin(j).wait_send()
 
@@ -347,26 +379,12 @@
     packed = jnp.concatenate([pno_basis, quarters], axis=1)
 
     t = jnp.arange(SLOTS, dtype=jnp.int32)
-    dz, dy, dx = t // 16, (t // 4) % 4, t % 4
-    source = ((zh + 4 - dz) % 4) * 16 + ((y + 4 - dy) % 4) * 4 + (x + 4 - dx) % 4
-    reads = couple.reshape(1, -1) == source[:, None]
-    readers = jnp.sum(jnp.where(reads, t[None, :] // 8, 0), axis=1)
-    scale = jnp.sum(jnp.where(reads, couple_weight.reshape(1, -1), 0.0), axis=1)
-    where = jnp.sum(jnp.where(reads, t[:, None], 0), axis=0)
-    target = ((zh + dz) % 4) * 16 + ((y + dy) % 4) * 4 + (x + dx) % 4
-    sends = jnp.sum(jnp.where(target[:, None] == t[None, :], send_list.reshape(1, -1), 0), axis=1)
-    tables = jnp.broadcast_to(jnp.pad(sends.reshape(4, 1, 16), ((0, 0), (0, 0), (0, 112))), (4, 8, 128))
-
-    j = jnp.arange(8, dtype=jnp.int32) // 2
-    bit = jnp.arange(8, dtype=jnp.int32) % 2
-    late = jnp.where(x < j, 1, 0)
-    stop_even, stop_odd = j + 4 * late, j + 4 * (1 - late)
-    stops = jnp.stack([jnp.where(zl == 0, stop_even, stop_odd), jnp.where(zl == 0, stop_odd, stop_even)])
-    column = stops * 2 + bit
-    chosen = jnp.sum(
-        jnp.where(column[:, None, :, None] == jnp.arange(16)[None, None, None, :], fit_weight[None, :, None, :], 0.0), axis=3
-    )
-    weights = jnp.broadcast_to(chosen.reshape(2, SLOTS, 1), (2, SLOTS, 128))
+    source = ((zh + 4 - t // 16) % 4) * 16 + ((y + 4 - (t // 4) % 4) % 4) * 4 + (x + 4 - t % 4) % 4
+    term = jnp.arange(PAIRS, dtype=jnp.int32)[:, None] * 8 + jnp.arange(8, dtype=jnp.int32)[None, :]
+    inverse = jnp.sum(jnp.where(couple[None] == source[:, None, None], term[None], 0), axis=(1, 2))
+    sends = send_list.reshape(SLOTS)
+    table = jnp.broadcast_to(jnp.pad(sends.reshape(1, SLOTS), ((0, 0), (0, 64))), (8, 128))
+    weights = jnp.pad(fit_weight, ((0, 0), (0, 112)))
 
     vmem, smem = pl.BlockSpec(memory_space=pltpu.VMEM), pl.BlockSpec(memory_space=pltpu.SMEM)
     tile = functools.partial(pltpu.VMEM, dtype=F32)
@@ -374,18 +392,18 @@
     out = pl.pallas_call(
         kernel,
         out_shape=jax.ShapeDtypeStruct((PAIRS, PNO, PNO), F32),
-        in_specs=[smem] * 4 + [vmem] * 4,
+        in_specs=[smem] * 5 + [vmem] * 4,
         out_specs=vmem,
         scratch_shapes=[
             tile((PAIRS, ROWS, ORB)), tile((PAIRS, ROWS, ORB)), tile((PAIRS, ROWS, ORB)),
             pltpu.VMEM((4, 8, 128), jnp.int32), pltpu.SMEM((4, 8, 128), jnp.int32),
             tile((SLOTS, ROWS, ORB)), tile((SLOTS, ROWS, ORB)),
             tile((2, 2, 2, 2, PNO, ORB)), tile((4, 2, 2, 2, 2, PNO, ORB)),
-            tile((PAIRS, PNO, ORB)), tile((SLOTS, 128)),
+            tile((PAIRS, PNO, ORB)), tile((PAIRS, 128)), pltpu.SMEM((PAIRS, 128), F32),
             narrow((PAIRS, PNO, ORB)), narrow((PAIRS, PNO, ORB)), narrow((PAIRS, PNO, ORB)), narrow((PAIRS, PNO, ORB)),
             narrow((4, ORB, ORB)), narrow((4, ORB, ORB)),
             narrow((4, PAIRS * PNO, ORB)), narrow((4, PAIRS * PNO, ORB)),
-            narrow((16, 512, PNO)), narrow((16, 512, PNO)), narrow((16, 512, PNO)), narrow((16, 512, PNO)),
+            narrow((16, 512, PNO)), narrow((16, 512, PNO)), narrow((16, PNO, 512)), narrow((16, PNO, 512)),
             tile((SLOTS, PNO, PNO)), tile((PAIRS, PNO, PNO)),
             tile((4, PNO, 128)), tile((4, PNO, 128)), tile((4, PNO, 128)), tile((4, PNO, 128)),
             pltpu.SemaphoreType.DMA((SLOTS,)), pltpu.SemaphoreType.DMA((SLOTS,)),
@@ -395,7 +413,7 @@
         compiler_params=pltpu.CompilerParams(
             collective_id=0, has_side_effects=True, vmem_limit_bytes=60 * 1024 * 1024
         ),
-    )(sends[:16], readers, where, scale, packed, fit_blocks, weights, tables)
+    )(sends, inverse, couple, couple_weight, fit_weight, packed, fit_blocks, weights, table)
     return out.reshape(PAIRS, PNO * PNO)
 
 

time: 218 us -> 173 us (0.79)
  Pallas kernels: 207 us -> 165 us
  other arithmetic: 4.15 us -> 1.63 us
    pallas_call x1, Pallas kernels: 207 us -> 165 us  [on_device(): pl.pallas_call(kernel, out_shape=jax.ShapeDtypeStruct((PAIRS, PNO, PNO),...]
    reduce_sum x4 -> x1, other arithmetic: 3.12 us -> 0.64 us  [on_device(): jnp.sum(jnp.where(couple[None] == source[:, None, None], term[None], 0),...]
where the time goes in v2:
time: 173 us
  Pallas kernels  165 us (95%)
  local copies, waits for them, and re-layouts  6.3 us (4%)
    pallas_call x1, Pallas kernels, on_device(): pl.pallas_call(kernel, out_shape=jax.ShapeDtypeStruct((PAIRS, PNO, PNO),...  165 us

profile of v2, /device:TPU:32, one launch (start us, length us, event | category | flops | bytes accessed | tf_op | source)
XLA Modules:
  0.0 172.5 jit_solution(4845656759321268744)
XLA Ops:
  0.0 0.0 copy-start.3
  0.0 0.6 copy-done.3
  0.7 0.0 copy-start.1
  0.7 0.1 iota_add_fusion
  0.8 0.6 copy-done.1
  1.4 0.6 select_reduce_fusion.inverse_ref
  2.0 0.0 copy-start.2
  2.0 0.6 broadcast_in_dim.27.table
  2.6 0.1 copy-done.2
  2.7 0.6 pad.8.weights
  3.3 1.0 reshape.117
  4.3 0.0 copy-start
  4.3 0.1 copy.11
  4.4 0.2 reshape.118
  4.6 0.7 copy-done
  5.3 0.9 pad_maximum_fusion.packed
  6.2 164.5 %shard_map.73 = f32[8,64,64]{2,1,0:T(8,128)} custom-call(s32[64]{0:T(128)} %bitcast.8, s32[64]{0:T(128)} %select_reduce_fusion.inverse_ref, s32[8,8]{1,0:T(8,128)} %couple_ref.1, f32[8,8]{1,0:T(8,128)} %scale_ref.1, f32[8,16]{1,0:T(8,128)} %rate_ref.1, f32[8,80,256]{2,1,0:T(8,128)} %pad_maximum_fusion.packed, f32[2,2,64,256]{3,2,1,0:T(8,128)} %shard.1, ...), custom_call_target="tpu_custom_call" | custom-call | tf_op jit(solution)/shard_map/pallas_call | solution.py:392
  170.8 1.7 reshape.119
  (3 shorter events, 0.0 us)
Async XLA Ops:
  0.0 0.7 copy-start.3
  0.7 0.7 copy-start.1
  2.0 0.7 copy-start.2
  4.3 1.0 copy-start

commit v3 on v2

--- a/solution.py
+++ b/solution.py
@@ -12,11 +12,12 @@
 PAIRS, PNO, ORB = 8, 64, 256
 ROWS = PNO + 16
 SLOTS = 64
-
-SHARD, BASES, WEIGHTS, TABLE, DSEND, PSEND, FY, CORE, UP, DOWN, RELAY, FX = (
-    0, 1, 2, 2, 6, 7, 8, 16, 20, 28, 36, 40,
+SHIFT = 3
+
+SHARD, BASES, WEIGHTS, TABLE, DSEND, PSEND, FY, CORE, UP, DOWN, RELAY, FX, DETOUR, ONWARD, SCALES, PARTS = (
+    0, 1, 2, 2, 6, 7, 8, 16, 20, 28, 36, 40, 56, 58, 59, 62,
 )
-TRANSFERS = 56
+TRANSFERS = 66
 NN = (((1,), (0,)), ((), ()))
 NT = (((1,), (1,)), ((), ()))
 
@@ -46,9 +47,9 @@
 
 def kernel(
     sends_ref, inverse_ref, couple_ref, scale_ref, rate_ref,
-    packed, shard, weights, table,
+    packed, shard, weights, table, scales,
     out_ref,
-    z1, z2, z3, tables_in, tables_sm, stage, arrived, whole, slots, partner_bases, partner_weights, partner_rates,
+    z1, z2, z3, detour, tables_in, tables_sm, scales_in, scales_sm, z_send, z_part, stage, arrived, whole, slots, partner_bases, partner_weights, partner_rates,
     basis_h, basis_l, other_h, other_l, block_h, block_l, proj_h, proj_l,
     f0_h, f0_l, f1_h, f1_l, terms, dressed, d_send, d_recv, part_send, part_recv,
     plane_send, plane_recv, send_sem, recv_sem, local_sem,
@@ -81,21 +82,37 @@
     bases = copy(BASES, packed.at[:, pl.ds(0, PNO), :], partner_bases, partner)
     wts = copy(WEIGHTS, weights, partner_weights, partner)
     tabs = {dz: copy(TABLE + dz, table, tables_in.at[dz], to) for dz, to in ((1, up), (2, across), (3, down))}
+    scls = {dz: copy(SCALES + dz, scales, scales_in.at[dz], to) for dz, to in ((1, up), (2, across), (3, down))}
+    back = {dz: copy(PARTS + dz, z_send.at[dz], z_part.at[dz], to) for dz, to in ((1, down), (2, across), (3, up))}
+    rows = pl.ds(0, PNO)
 
     def z_up(i):
-        return copy(UP + i, packed.at[i], z1.at[i], up)
+        return copy(UP + i, packed.at[i, rows], z1.at[i], up)
 
     def z_down(i):
-        return copy(DOWN + i, packed.at[i], z3.at[i], down)
-
-    def relay(i):
-        if i < 4:
-            return copy(RELAY + i, z1.at[i], z2.at[i], up)
+        return copy(DOWN + i, packed.at[i, rows], z3.at[i], down)
+
+    def relay_up(i):
+        return copy(RELAY + i, z1.at[i], z2.at[i], up)
+
+    def relay_down(i):
         return copy(RELAY + i, z3.at[i], z2.at[i], down)
 
     def fy(a):
         return copy(FY + a, whole.at[0, a], whole.at[1, a], fit_to)
 
+
+    def aside(a):
+        return copy(DETOUR + a, whole.at[0, a], detour.at[a], device(zh, 1, x, zl, core))
+
+    def onward(a):
+        return pltpu.make_async_remote_copy(
+            src_ref=detour.at[a], dst_ref=whole.at[1, a], send_sem=send_sem.at[ONWARD + a], recv_sem=recv_sem.at[FY + a],
+            device_id=up, device_id_type=MESH,
+        )
+
+    turns = (1 - zl) * lax.div(y, 3)
+    bends = (1 - zl) * lax.rem(y, 2) * (1 - lax.div(y, 3))
 
     def fx(dx, which, i):
         a, k = i // 2, i % 2
@@ -118,14 +135,15 @@
         pltpu.make_async_copy(whole.at[which], slots.at[0, :, core], local_sem.at[1]).start()
         copy(CORE, whole.at[which], slots.at[0, :, core], twin).start()
 
-    def reader_of(t):
-        return (zh * 4 + lax.rem(y + lax.div(t, 4), 4)) * 4 + lax.rem(x + lax.rem(t, 4), 4)
-
-    def fill_stage(source, index_of, dz):
-        arrived[dz * 16] = source[index_of(0)]
+    def fill_stage(dz):
+        def picked(t):
+            group = lax.rem(zh + 4 - dz, 4) * 4 + lax.rem(y + lax.div(t, 4), 4)
+            return packed[sends_ref[group * 4 + lax.rem(x + lax.rem(t, 4), 4)]]
+
+        arrived[dz * 16] = picked(0)
 
         def one(t, _):
-            stage[dz * 16 + t] = source[index_of(t)]
+            stage[dz * 16 + t] = picked(t)
             return 0
 
         lax.fori_loop(1, 16, one, 0)
@@ -148,10 +166,11 @@
         greet(to)
     own_shard = pltpu.make_async_copy(shard, whole.at[0, zl], local_sem.at[0])
     own_shard.start()
-    fill_stage(packed, lambda t: sends_ref[reader_of(t)], 0)
+    for dz in (1, 3, 2, 0):
+        fill_stage(dz)
 
     def split_own(p, _):
-        basis_h[p], basis_l[p] = split(packed[p, :PNO, :])
+        basis_h[0, p], basis_l[0, p] = split(packed[p, :PNO, :])
         return 0
 
     lax.fori_loop(0, PAIRS, split_own, 0)
@@ -159,51 +178,93 @@
     pl.semaphore_wait(barrier, 22)
 
     sh.start()
-    for t in (1, 4, 3, 12, 5, 7, 13, 15):
-        plane_copy(0, t).start()
-
-    sh.wait_recv()
-    fy(0).start()
-    fy(1).start()
     for dz in (1, 3, 2):
         tabs[dz].start()
+        scls[dz].start()
     for i in range(4):
         z_up(i).start()
         z_down(4 + i).start()
-    for t in (2, 8, 6, 9, 14, 11, 10):
-        plane_copy(0, t).start()
-
-    @pl.when(zl == 0)
-    def _():
-        first_slot(0)
+    send_stage(1)
+
+    sh.wait_recv()
+
+    @pl.when(turns == 1)
+    def _():
+        aside(0).start()
+        aside(1).start()
+
+    @pl.when(turns == 0)
+    def _():
+        fy(0).start()
+        fy(1).start()
 
     def own_rows(dx):
         return (1 - zl) * (1 - lax.div(x + dx, 4))
 
     for i in range(4):
         z_up(4 + i).start()
-        z_down(i).start()
+        z_down(3 - i).start()
         send_rows(0, (i,))
+
+    @pl.when(zl == 0)
+    def _():
+        first_slot(0)
+
+    send_stage(3)
+
+    @pl.when(bends == 1)
+    def _():
+        for a in range(2):
+            aside(a).wait_recv()
+            onward(a).start()
+
     fy(0).wait_recv()
     fy(1).wait_recv()
     for i in range(4):
         z_up(i).wait_recv()
-        relay(i).start()
+        if i < SHIFT:
+            relay_up(i).start()
+        else:
+
+            @pl.when(y == 0)
+            def _():
+                relay_up(i).start()
+
         z_down(4 + i).wait_recv()
-        relay(4 + i).start()
+        relay_down(4 + i).start()
         send_rows(1, (i,))
 
     @pl.when(zl == 1)
     def _():
         first_slot(1)
 
-    def pass_on(dz, source):
+    send_stage(2)
+    wts.start()
+    bases.start()
+    send_stage(0)
+    for i in (3, 2, 1, 0):
+        z_down(i).wait_recv()
+        if i >= SHIFT:
+
+            @pl.when(y > 0)
+            def _():
+                relay_down(i).start()
+
+    def readers(dz, source):
         tabs[dz].wait_recv()
-        table = pltpu.make_async_copy(tables_in.at[dz], tables_sm.at[dz], local_sem.at[1 + dz])
-        table.start()
-        table.wait()
-        fill_stage(source, lambda t: tables_sm[dz, 0, reader_of(t)], dz)
-        send_stage(dz)
+        scls[dz].wait_recv()
+        table_in = pltpu.make_async_copy(tables_in.at[dz], tables_sm.at[dz], local_sem.at[2])
+        scale_in = pltpu.make_async_copy(scales_in.at[dz], scales_sm.at[dz], local_sem.at[3])
+        table_in.start()
+        scale_in.start()
+
+        def one(p, _):
+            basis_h[dz, p], basis_l[dz, p] = split(source[p])
+            return 0
+
+        lax.fori_loop(0, PAIRS, one, 0)
+        table_in.wait()
+        scale_in.wait()
 
     def dress(dz):
         def one_of(t):
@@ -220,19 +281,38 @@
 
         def some(i, _):
             for u in range(4):
-                t = dz * 16 + i * 4 + u
-                term = inverse_ref[t]
+                t = i * 4 + u
+                term = inverse_ref[t] if dz == 0 else tables_sm[dz, 8, (4 - dz) * 16 + t]
                 reader, of = lax.div(term, 8), lax.rem(term, 8)
-                own = basis_h[reader], basis_l[reader]
-                overlap = split(dot3(own, split(arrived[t, :PNO, :]), NT))
-                half = split(dot3(overlap, split(natural(arrived[t, PNO:, :])), NN))
-                terms[t] = scale_ref[reader, of] * dot3(half, overlap, NT)
+                scale = scale_ref[reader, of] if dz == 0 else scales_sm[dz, reader, of]
+                own = basis_h[dz, reader], basis_l[dz, reader]
+                n = dz * 16 + t
+                overlap = split(dot3(own, split(arrived[n, :PNO, :]), NT))
+                half = split(dot3(overlap, split(natural(arrived[n, PNO:, :])), NN))
+                terms[n] = scale * dot3(half, overlap, NT)
             return 0
 
         lax.fori_loop(0, 4, some, 0)
 
+    def part(dz, p):
+        total = jnp.zeros((PNO, PNO), F32)
+        for c in range(8):
+            slot = couple_ref[p, c] if dz == 0 else tables_sm[dz, p, c]
+            here = jnp.where(lax.div(slot, 16) == zh, 1.0, 0.0)
+            row = lax.rem(y + 4 - lax.rem(lax.div(slot, 4), 4), 4)
+            total = total + here * terms[dz * 16 + row * 4 + lax.rem(x + 4 - lax.rem(slot, 4), 4)]
+        return total
+
+    def give_back(dz):
+        def one(q, _):
+            z_send[dz, q] = jnp.concatenate([part(dz, q), part(dz, q + 4)], axis=1)
+            return 0
+
+        lax.fori_loop(0, 4, one, 0)
+        back[dz].start()
+
     def fit(j, group):
-        bases_h, bases_l = (basis_h, basis_l) if group == 0 else (other_h, other_l)
+        bases_h, bases_l = (basis_h.at[0], basis_l.at[0]) if group == 0 else (other_h, other_l)
         rates = rate_ref if group == 0 else partner_rates
         late = lax.div(3 - x + j, 4)
         stop = j + 4 * (zl + late - 2 * zl * late)
@@ -266,20 +346,14 @@
 
     for i in range(4):
         z_up(4 + i).wait_recv()
-    pass_on(1, z1)
-    for i in range(4):
-        z_down(i).wait_recv()
-    pass_on(3, z3)
-    wts.start()
-    bases.start()
-    dress(0)
+    readers(1, z1)
+    readers(3, z3)
+    dress(1)
+    give_back(1)
     to_twin(0).wait_recv()
     pltpu.make_async_copy(whole.at[0], slots.at[0, :, core], local_sem.at[1]).wait()
     load_blocks(0)
     fit(0, 0)
-    for i in range(8):
-        relay(i).wait_recv()
-    pass_on(2, z2)
     for dx in (1, 3, 2):
         for i in range(4):
             fx(dx, 0, i).wait_recv()
@@ -296,25 +370,39 @@
 
     lax.fori_loop(0, PAIRS, split_other, 0)
     fit(0, 1)
-    dress(1)
     dress(3)
-    for j in (1, 3, 2):
+    give_back(3)
+    for i in range(8):
+        relay_up(i).wait_recv()
+    readers(2, z2)
+    for j in (1, 3):
         to_twin(j).wait_recv()
         load_blocks(j)
         fit(j, 0)
         fit(j, 1)
     dress(2)
+    give_back(2)
+    to_twin(2).wait_recv()
+    load_blocks(2)
+    fit(2, 0)
+    fit(2, 1)
+    dress(0)
 
     def gather_terms(p, _):
-        total = natural(packed[p, PNO:, :])
-        for c in range(8):
-            slot = couple_ref[p, c]
-            back = lax.rem(zh + 4 - lax.div(slot, 16), 4) * 16 + lax.rem(y + 4 - lax.rem(lax.div(slot, 4), 4), 4) * 4
-            total = total + terms[back + lax.rem(x + 4 - lax.rem(slot, 4), 4)]
-        dressed[p] = total
+        dressed[p] = natural(packed[p, PNO:, :]) + part(0, p)
         return 0
 
     lax.fori_loop(0, PAIRS, gather_terms, 0)
+    for dz in (1, 3, 2):
+        back[dz].wait_recv()
+
+    def gather_parts(q, _):
+        two = z_part[1, q] + z_part[2, q] + z_part[3, q]
+        dressed[q] = dressed[q] + two[:, :PNO]
+        dressed[q + 4] = dressed[q + 4] + two[:, PNO:]
+        return 0
+
+    lax.fori_loop(0, 4, gather_parts, 0)
     for q in range(4):
         d_send[q] = jnp.concatenate([dressed[q], dressed[q + 4]], axis=1)
     ds = copy(DSEND, d_send, d_recv, partner)
@@ -346,12 +434,28 @@
     ps = copy(PSEND, part_send, part_recv, partner)
     ps.start()
 
-    for done in (sh, bases, wts, fy(0), fy(1), ds, *tabs.values()):
+    for done in (sh, bases, wts, ds, *tabs.values(), *scls.values(), *back.values()):
         done.wait_send()
+
+    @pl.when(turns == 1)
+    def _():
+        aside(0).wait_send()
+        aside(1).wait_send()
+
+    @pl.when(turns == 0)
+    def _():
+        fy(0).wait_send()
+        fy(1).wait_send()
+
+    @pl.when(bends == 1)
+    def _():
+        onward(0).wait_send()
+        onward(1).wait_send()
+
     for i in range(8):
         z_up(i).wait_send()
         z_down(i).wait_send()
-        relay(i).wait_send()
+        relay_up(i).wait_send()
     for dx in (1, 2, 3):
         for i in range(4):
             fx(dx, 0, i).wait_send()
@@ -383,7 +487,10 @@
     term = jnp.arange(PAIRS, dtype=jnp.int32)[:, None] * 8 + jnp.arange(8, dtype=jnp.int32)[None, :]
     inverse = jnp.sum(jnp.where(couple[None] == source[:, None, None], term[None], 0), axis=(1, 2))
     sends = send_list.reshape(SLOTS)
-    table = jnp.broadcast_to(jnp.pad(sends.reshape(1, SLOTS), ((0, 0), (0, 64))), (8, 128))
+    table = jnp.concatenate(
+        [jnp.pad(couple, ((0, 0), (0, 120))), jnp.broadcast_to(jnp.pad(inverse.reshape(1, SLOTS), ((0, 0), (0, 64))), (8, 128))]
+    )
+    scales = jnp.pad(couple_weight, ((0, 0), (0, 120)))
     weights = jnp.pad(fit_weight, ((0, 0), (0, 112)))
 
     vmem, smem = pl.BlockSpec(memory_space=pltpu.VMEM), pl.BlockSpec(memory_space=pltpu.SMEM)
@@ -392,15 +499,17 @@
     out = pl.pallas_call(
         kernel,
         out_shape=jax.ShapeDtypeStruct((PAIRS, PNO, PNO), F32),
-        in_specs=[smem] * 5 + [vmem] * 4,
+        in_specs=[smem] * 5 + [vmem] * 5,
         out_specs=vmem,
         scratch_shapes=[
-            tile((PAIRS, ROWS, ORB)), tile((PAIRS, ROWS, ORB)), tile((PAIRS, ROWS, ORB)),
-            pltpu.VMEM((4, 8, 128), jnp.int32), pltpu.SMEM((4, 8, 128), jnp.int32),
+            tile((PAIRS, PNO, ORB)), tile((PAIRS, PNO, ORB)), tile((PAIRS, PNO, ORB)),
+            tile((2, 2, 2, PNO, ORB)),
+            pltpu.VMEM((4, 16, 128), jnp.int32), pltpu.SMEM((4, 16, 128), jnp.int32),
+            tile((4, 8, 128)), pltpu.SMEM((4, 8, 128), F32), tile((4, 4, PNO, 128)), tile((4, 4, PNO, 128)),
             tile((SLOTS, ROWS, ORB)), tile((SLOTS, ROWS, ORB)),
             tile((2, 2, 2, 2, PNO, ORB)), tile((4, 2, 2, 2, 2, PNO, ORB)),
             tile((PAIRS, PNO, ORB)), tile((PAIRS, 128)), pltpu.SMEM((PAIRS, 128), F32),
-            narrow((PAIRS, PNO, ORB)), narrow((PAIRS, PNO, ORB)), narrow((PAIRS, PNO, ORB)), narrow((PAIRS, PNO, ORB)),
+            narrow((4, PAIRS, PNO, ORB)), narrow((4, PAIRS, PNO, ORB)), narrow((PAIRS, PNO, ORB)), narrow((PAIRS, PNO, ORB)),
             narrow((4, ORB, ORB)), narrow((4, ORB, ORB)),
             narrow((4, PAIRS * PNO, ORB)), narrow((4, PAIRS * PNO, ORB)),
             narrow((16, 512, PNO)), narrow((16, 512, PNO)), narrow((16, PNO, 512)), narrow((16, PNO, 512)),
@@ -413,7 +522,7 @@
         compiler_params=pltpu.CompilerParams(
             collective_id=0, has_side_effects=True, vmem_limit_bytes=60 * 1024 * 1024
         ),
-    )(sends, inverse, couple, couple_weight, fit_weight, packed, fit_blocks, weights, table)
+    )(sends, inverse, couple, couple_weight, fit_weight, packed, fit_blocks, weights, table, scales)
     return out.reshape(PAIRS, PNO * PNO)
 
 

time: 173 us -> 152 us (0.88)
  Pallas kernels: 165 us -> 143 us
    pallas_call x1, Pallas kernels: 165 us -> 143 us  [on_device(): pl.pallas_call(kernel, out_shape=jax.ShapeDtypeStruct((PAIRS, PNO, PNO),...]
where the time goes in v3:
time: 152 us; the launch traced here: 151 us
  Pallas kernels  143 us (94%)
  local copies, waits for them, and re-layouts  6.21 us (4%)
  other arithmetic  1.68 us (1%)
    pallas_call x1, Pallas kernels, on_device(): pl.pallas_call(kernel, out_shape=jax.ShapeDtypeStruct((PAIRS, PNO, PNO),...  143 us

profile of v3, /device:TPU:32, one launch (start us, length us, event | category | flops | bytes accessed | tf_op | source)
XLA Modules:
  0.0 151.3 jit_solution(3657700821769196152)
XLA Ops:
  0.0 0.0 copy-start.1
  0.0 0.1 iota_add_fusion
  0.1 0.6 copy-done.1
  0.7 0.1 select_reduce_fusion.inverse_ref
  0.8 0.0 copy-start.4
  0.8 0.5 copy-done.4
  1.3 0.0 copy-start.2
  1.3 0.6 pad_add_fusion.table
  1.9 0.1 copy-done.2
  2.0 0.0 copy-start.3
  2.0 0.6 pad.19.scales
  2.6 0.1 copy-done.3
  2.7 0.6 pad.16.weights
  3.3 1.0 reshape.120
  4.3 0.0 copy-start
  4.3 0.1 copy.11
  4.4 0.2 reshape.121
  4.6 0.7 copy-done
  5.3 0.9 pad_maximum_fusion.packed
  6.2 143.4 %shard_map.73 = f32[8,64,64]{2,1,0:T(8,128)} custom-call(s32[64]{0:T(128)} %bitcast.9, s32[64]{0:T(128)} %copy-done.4, s32[8,8]{1,0:T(8,128)} %couple_ref.1, f32[8,8]{1,0:T(8,128)} %scale_ref.1, f32[8,16]{1,0:T(8,128)} %rate_ref.1, f32[8,80,256]{2,1,0:T(8,128)} %pad_maximum_fusion.packed, f32[2,2,64,256]{3,2,1,0:T(8,128)} %shard.1, f32[8,128]{1,0:T(8,128)} %pad.16.weights, ...), custom_call_target="tpu_custom_call" | custom-call | tf_op jit(solution)/shard_map/pallas_call | solution.py:499
  149.6 1.7 %reshape.123 = f32[8,4096]{1,0:T(8,128)} reshape(f32[8,64,64]{2,1,0:T(8,128)} %shard_map.73) | data formatting | bytes 262144 | tf_op jit(solution)/shard_map/reshape | solution.py:526
  (4 shorter events, 0.0 us)
Async XLA Ops:
  0.0 0.7 copy-start.1
  0.8 0.5 copy-start.4
  1.3 0.7 copy-start.2
  2.0 0.7 copy-start.3
  4.3 1.0 copy-start

commit v4 on v3

--- a/solution.py
+++ b/solution.py
@@ -184,7 +184,7 @@
     for i in range(4):
         z_up(i).start()
         z_down(4 + i).start()
-    send_stage(1)
+    send_stage(0)
 
     sh.wait_recv()
 
@@ -210,45 +210,13 @@
     def _():
         first_slot(0)
 
-    send_stage(3)
+    send_stage(1)
 
     @pl.when(bends == 1)
     def _():
         for a in range(2):
             aside(a).wait_recv()
             onward(a).start()
-
-    fy(0).wait_recv()
-    fy(1).wait_recv()
-    for i in range(4):
-        z_up(i).wait_recv()
-        if i < SHIFT:
-            relay_up(i).start()
-        else:
-
-            @pl.when(y == 0)
-            def _():
-                relay_up(i).start()
-
-        z_down(4 + i).wait_recv()
-        relay_down(4 + i).start()
-        send_rows(1, (i,))
-
-    @pl.when(zl == 1)
-    def _():
-        first_slot(1)
-
-    send_stage(2)
-    wts.start()
-    bases.start()
-    send_stage(0)
-    for i in (3, 2, 1, 0):
-        z_down(i).wait_recv()
-        if i >= SHIFT:
-
-            @pl.when(y > 0)
-            def _():
-                relay_down(i).start()
 
     def readers(dz, source):
         tabs[dz].wait_recv()
@@ -336,7 +304,7 @@
             f1_h[n, :, pl.ds(j * 128, 128)], f1_l[n, :, pl.ds(j * 128, 128)] = split(right)
             return 0
 
-        lax.fori_loop(0, PAIRS, pair, 0)
+        lax.fori_loop(0, PAIRS, pair, 0, unroll=4)
 
     def load_blocks(j):
         for n in range(4):
@@ -344,25 +312,63 @@
             rows = [slots[j, a, b, k, m] for a in range(2) for b in range(2)]
             block_h[n], block_l[n] = split(jnp.concatenate(rows, axis=0))
 
+    dress(0)
+    fy(0).wait_recv()
+    fy(1).wait_recv()
+    for i in range(4):
+        z_up(i).wait_recv()
+        if i < SHIFT:
+            relay_up(i).start()
+        else:
+
+            @pl.when(y == 0)
+            def _():
+                relay_up(i).start()
+
+        z_down(4 + i).wait_recv()
+        relay_down(4 + i).start()
+        send_rows(1, (i,))
+
+    @pl.when(zl == 1)
+    def _():
+        first_slot(1)
+
+    send_stage(3)
+    wts.start()
+    bases.start()
+    send_stage(2)
+    for i in (3, 2, 1, 0):
+        z_down(i).wait_recv()
+        if i >= SHIFT:
+
+            @pl.when(y > 0)
+            def _():
+                relay_down(i).start()
+
+    to_twin(0).wait_recv()
+    pltpu.make_async_copy(whole.at[0], slots.at[0, :, core], local_sem.at[1]).wait()
+    load_blocks(0)
+    fit(0, 0)
     for i in range(4):
         z_up(4 + i).wait_recv()
     readers(1, z1)
     readers(3, z3)
+    for dx in (1, 3):
+        for i in range(4):
+            fx(dx, 0, i).wait_recv()
+        to_twin(dx).start()
     dress(1)
     give_back(1)
-    to_twin(0).wait_recv()
-    pltpu.make_async_copy(whole.at[0], slots.at[0, :, core], local_sem.at[1]).wait()
-    load_blocks(0)
-    fit(0, 0)
-    for dx in (1, 3, 2):
+    for dx in (2,):
         for i in range(4):
             fx(dx, 0, i).wait_recv()
         to_twin(dx).start()
     wts.wait_recv()
     rates_in = pltpu.make_async_copy(partner_weights, partner_rates, local_sem.at[1])
     rates_in.start()
+    to_twin(1).wait_recv()
+    rates_in.wait()
     bases.wait_recv()
-    rates_in.wait()
 
     def split_other(p, _):
         other_h[p], other_l[p] = split(partner_bases[p])
@@ -370,23 +376,24 @@
 
     lax.fori_loop(0, PAIRS, split_other, 0)
     fit(0, 1)
+    load_blocks(1)
+    fit(1, 0)
+    fit(1, 1)
     dress(3)
     give_back(3)
     for i in range(8):
         relay_up(i).wait_recv()
     readers(2, z2)
-    for j in (1, 3):
-        to_twin(j).wait_recv()
-        load_blocks(j)
-        fit(j, 0)
-        fit(j, 1)
+    to_twin(3).wait_recv()
+    load_blocks(3)
+    fit(3, 0)
+    fit(3, 1)
     dress(2)
     give_back(2)
     to_twin(2).wait_recv()
     load_blocks(2)
     fit(2, 0)
     fit(2, 1)
-    dress(0)
 
     def gather_terms(p, _):
         dressed[p] = natural(packed[p, PNO:, :]) + part(0, p)
@@ -420,7 +427,7 @@
         dressed[p] = dressed[p] + fitted_sum(p, dressed[p])
         return 0
 
-    lax.fori_loop(0, PAIRS, finish_own, 0)
+    lax.fori_loop(0, PAIRS, finish_own, 0, unroll=4)
     ds.wait_recv()
 
     def finish_other(q, _):
@@ -430,7 +437,7 @@
         )
         return 0
 
-    lax.fori_loop(0, 4, finish_other, 0)
+    lax.fori_loop(0, 4, finish_other, 0, unroll=4)
     ps = copy(PSEND, part_send, part_recv, partner)
     ps.start()
 

time: 152 us -> 145 us (0.954)
  Pallas kernels: 143 us -> 135 us
    pallas_call x1, Pallas kernels: 143 us -> 135 us  [on_device(): pl.pallas_call(kernel, out_shape=jax.ShapeDtypeStruct((PAIRS, PNO, PNO),...]
where the time goes in v4:
time: 145 us; the launch traced here: 143 us
  Pallas kernels  135 us (93%)
  local copies, waits for them, and re-layouts  6.21 us (4%)
  other arithmetic  1.68 us (1%)
    pallas_call x1, Pallas kernels, on_device(): pl.pallas_call(kernel, out_shape=jax.ShapeDtypeStruct((PAIRS, PNO, PNO),...  135 us

profile of v4, /device:TPU:32, one launch (start us, length us, event | category | flops | bytes accessed | tf_op | source)
XLA Modules:
  0.0 143.1 jit_solution(8465856941610632112)
XLA Ops:
  0.0 0.0 copy-start.1
  0.0 0.1 iota_add_fusion
  0.1 0.6 copy-done.1
  0.7 0.1 select_reduce_fusion.inverse_ref
  0.8 0.0 copy-start.4
  0.8 0.5 copy-done.4
  1.3 0.0 copy-start.2
  1.3 0.6 pad_add_fusion.table
  1.9 0.1 copy-done.2
  2.0 0.0 copy-start.3
  2.0 0.6 pad.19.scales
  2.6 0.1 copy-done.3
  2.7 0.6 pad.16.weights
  3.3 1.0 reshape.120
  4.3 0.0 copy-start
  4.3 0.1 copy.11
  4.4 0.2 reshape.121
  4.6 0.7 copy-done
  5.3 0.9 pad_maximum_fusion.packed
  6.2 135.1 %shard_map.73 = f32[8,64,64]{2,1,0:T(8,128)} custom-call(s32[64]{0:T(128)} %bitcast.9, s32[64]{0:T(128)} %copy-done.4, s32[8,8]{1,0:T(8,128)} %couple_ref.1, f32[8,8]{1,0:T(8,128)} %scale_ref.1, f32[8,16]{1,0:T(8,128)} %rate_ref.1, f32[8,80,256]{2,1,0:T(8,128)} %pad_maximum_fusion.packed, f32[2,2,64,256]{3,2,1,0:T(8,128)} %shard.1, f32[8,128]{1,0:T(8,128)} %pad.16.weights, ...), custom_call_target="tpu_custom_call" | custom-call | tf_op jit(solution)/shard_map/pallas_call | solution.py:506
  141.3 1.7 %reshape.123 = f32[8,4096]{1,0:T(8,128)} reshape(f32[8,64,64]{2,1,0:T(8,128)} %shard_map.73) | data formatting | bytes 262144 | tf_op jit(solution)/shard_map/reshape | solution.py:533
  (4 shorter events, 0.0 us)
Async XLA Ops:
  0.0 0.7 copy-start.1
  0.8 0.5 copy-start.4
  1.3 0.7 copy-start.2
  2.0 0.7 copy-start.3
  4.3 1.0 copy-start

commit v5 on v4

--- a/solution.py
+++ b/solution.py
@@ -14,10 +14,11 @@
 SLOTS = 64
 SHIFT = 3
 
-SHARD, BASES, WEIGHTS, TABLE, DSEND, PSEND, FY, CORE, UP, DOWN, RELAY, FX, DETOUR, ONWARD, SCALES, PARTS = (
-    0, 1, 2, 2, 6, 7, 8, 16, 20, 28, 36, 40, 56, 58, 59, 62,
+SHARD, BASES, WEIGHTS, TABLE, FY, CORE, UP, DOWN, RELAY, FX, DETOUR, ONWARD, SCALES, PARTS = (
+    0, 1, 2, 2, 8, 16, 20, 28, 36, 40, 56, 58, 59, 62,
 )
-TRANSFERS = 66
+DSEND, PSEND = (6, 7, 66, 67), (68, 69, 70, 71)
+TRANSFERS = 72
 NN = (((1,), (0,)), ((), ()))
 NT = (((1,), (1,)), ((), ()))
 
@@ -248,8 +249,8 @@
         lax.fori_loop(dz * 16 + 1, dz * 16 + 16, arrive, 0)
 
         def some(i, _):
-            for u in range(4):
-                t = i * 4 + u
+            for u in range(8):
+                t = i * 8 + u
                 term = inverse_ref[t] if dz == 0 else tables_sm[dz, 8, (4 - dz) * 16 + t]
                 reader, of = lax.div(term, 8), lax.rem(term, 8)
                 scale = scale_ref[reader, of] if dz == 0 else scales_sm[dz, reader, of]
@@ -260,7 +261,7 @@
                 terms[n] = scale * dot3(half, overlap, NT)
             return 0
 
-        lax.fori_loop(0, 4, some, 0)
+        lax.fori_loop(0, 2, some, 0)
 
     def part(dz, p):
         total = jnp.zeros((PNO, PNO), F32)
@@ -412,8 +413,10 @@
     lax.fori_loop(0, 4, gather_parts, 0)
     for q in range(4):
         d_send[q] = jnp.concatenate([dressed[q], dressed[q + 4]], axis=1)
-    ds = copy(DSEND, d_send, d_recv, partner)
-    ds.start()
+    ds = [copy(DSEND[q], d_send.at[q], d_recv.at[q], partner) for q in range(4)]
+    ps = [copy(PSEND[q], part_send.at[q], part_recv.at[q], partner) for q in range(4)]
+    for q in range(4):
+        ds[q].start()
 
     def fitted_sum(n, d):
         left = dot3((f0_h[n], f0_l[n]), split(d), NN)
@@ -428,20 +431,15 @@
         return 0
 
     lax.fori_loop(0, PAIRS, finish_own, 0, unroll=4)
-    ds.wait_recv()
-
-    def finish_other(q, _):
+    for q in range(4):
+        ds[q].wait_recv()
         two = d_recv[q]
         part_send[q] = jnp.concatenate(
             [fitted_sum(PAIRS + q, two[:, :PNO]), fitted_sum(PAIRS + q + 4, two[:, PNO:])], axis=1
         )
-        return 0
-
-    lax.fori_loop(0, 4, finish_other, 0, unroll=4)
-    ps = copy(PSEND, part_send, part_recv, partner)
-    ps.start()
-
-    for done in (sh, bases, wts, ds, *tabs.values(), *scls.values(), *back.values()):
+        ps[q].start()
+
+    for done in (sh, bases, wts, *ds, *tabs.values(), *scls.values(), *back.values()):
         done.wait_send()
 
     @pl.when(turns == 1)
@@ -477,8 +475,8 @@
         return 0
 
     lax.fori_loop(0, SLOTS, plane_sent, 0)
-    ps.wait()
     for q in range(4):
+        ps[q].wait()
         two = part_recv[q]
         out_ref[q] = dressed[q] + two[:, :PNO]
         out_ref[q + 4] = dressed[q + 4] + two[:, PNO:]

time: 145 us -> 142 us (0.979)
  Pallas kernels: 135 us -> 133 us
    pallas_call x1, Pallas kernels: 135 us -> 133 us  [on_device(): pl.pallas_call(kernel, out_shape=jax.ShapeDtypeStruct((PAIRS, PNO, PNO),...]
where the time goes in v5:
time: 142 us; the launch traced here: 141 us
  Pallas kernels  133 us (94%)
  local copies, waits for them, and re-layouts  6.21 us (4%)
  other arithmetic  1.68 us (1%)
    pallas_call x1, Pallas kernels, on_device(): pl.pallas_call(kernel, out_shape=jax.ShapeDtypeStruct((PAIRS, PNO, PNO),...  133 us

profile of v5, /device:TPU:32, one launch (start us, length us, event | category | flops | bytes accessed | tf_op | source)
XLA Modules:
  0.0 141.3 jit_solution(9242404204128236666)
XLA Ops:
  0.0 0.0 copy-start.1
  0.0 0.1 iota_add_fusion
  0.1 0.6 copy-done.1
  0.7 0.1 select_reduce_fusion.inverse_ref
  0.8 0.0 copy-start.4
  0.8 0.5 copy-done.4
  1.3 0.0 copy-start.2
  1.3 0.6 pad_add_fusion.table
  1.9 0.1 copy-done.2
  2.0 0.0 copy-start.3
  2.0 0.6 pad.19.scales
  2.6 0.1 copy-done.3
  2.7 0.6 pad.16.weights
  3.3 1.0 reshape.120
  4.3 0.0 copy-start
  4.3 0.1 copy.11
  4.4 0.2 reshape.121
  4.6 0.7 copy-done
  5.3 0.9 pad_maximum_fusion.packed
  6.2 133.4 %shard_map.73 = f32[8,64,64]{2,1,0:T(8,128)} custom-call(s32[64]{0:T(128)} %bitcast.9, s32[64]{0:T(128)} %copy-done.4, s32[8,8]{1,0:T(8,128)} %couple_ref.1, f32[8,8]{1,0:T(8,128)} %scale_ref.1, f32[8,16]{1,0:T(8,128)} %rate_ref.1, f32[8,80,256]{2,1,0:T(8,128)} %pad_maximum_fusion.packed, f32[2,2,64,256]{3,2,1,0:T(8,128)} %shard.1, f32[8,128]{1,0:T(8,128)} %pad.16.weights, ...), custom_call_target="tpu_custom_call" | custom-call | tf_op jit(solution)/shard_map/pallas_call | solution.py:504
  139.6 1.7 %reshape.123 = f32[8,4096]{1,0:T(8,128)} reshape(f32[8,64,64]{2,1,0:T(8,128)} %shard_map.73) | data formatting | bytes 262144 | tf_op jit(solution)/shard_map/reshape | solution.py:531
  (4 shorter events, 0.0 us)
Async XLA Ops:
  0.0 0.7 copy-start.1
  0.8 0.5 copy-start.4
  1.3 0.7 copy-start.2
  2.0 0.7 copy-start.3
  4.3 1.0 copy-start

commit v6 on v5

--- a/solution.py
+++ b/solution.py
@@ -277,7 +277,7 @@
             z_send[dz, q] = jnp.concatenate([part(dz, q), part(dz, q + 4)], axis=1)
             return 0
 
-        lax.fori_loop(0, 4, one, 0)
+        lax.fori_loop(0, 4, one, 0, unroll=2)
         back[dz].start()
 
     def fit(j, group):
@@ -400,7 +400,7 @@
         dressed[p] = natural(packed[p, PNO:, :]) + part(0, p)
         return 0
 
-    lax.fori_loop(0, PAIRS, gather_terms, 0)
+    lax.fori_loop(0, PAIRS, gather_terms, 0, unroll=4)
     for dz in (1, 3, 2):
         back[dz].wait_recv()
 
@@ -410,7 +410,7 @@
         dressed[q + 4] = dressed[q + 4] + two[:, PNO:]
         return 0
 
-    lax.fori_loop(0, 4, gather_parts, 0)
+    lax.fori_loop(0, 4, gather_parts, 0, unroll=4)
     for q in range(4):
         d_send[q] = jnp.concatenate([dressed[q], dressed[q + 4]], axis=1)
     ds = [copy(DSEND[q], d_send.at[q], d_recv.at[q], partner) for q in range(4)]
@@ -430,7 +430,7 @@
         dressed[p] = dressed[p] + fitted_sum(p, dressed[p])
         return 0
 
-    lax.fori_loop(0, PAIRS, finish_own, 0, unroll=4)
+    lax.fori_loop(0, PAIRS, finish_own, 0, unroll=8)
     for q in range(4):
         ds[q].wait_recv()
         two = d_recv[q]

time: 142 us -> 142 us (level)
  no operation moved by 1% of the time
where the time goes in v6:
time: 142 us; the launch traced here: 141 us
  Pallas kernels  133 us (94%)
  local copies, waits for them, and re-layouts  6.21 us (4%)
  other arithmetic  1.68 us (1%)
    pallas_call x1, Pallas kernels, on_device(): pl.pallas_call(kernel, out_shape=jax.ShapeDtypeStruct((PAIRS, PNO, PNO),...  133 us

profile of v6, /device:TPU:32, one launch (start us, length us, event | category | flops | bytes accessed | tf_op | source)
XLA Modules:
  0.0 140.9 jit_solution(12696161457003411787)
XLA Ops:
  0.0 0.0 copy-start.1
  0.0 0.1 iota_add_fusion
  0.1 0.6 copy-done.1
  0.7 0.1 select_reduce_fusion.inverse_ref
  0.8 0.0 copy-start.4
  0.8 0.5 copy-done.4
  1.3 0.0 copy-start.2
  1.3 0.6 pad_add_fusion.table
  1.9 0.1 copy-done.2
  2.0 0.0 copy-start.3
  2.0 0.6 pad.19.scales
  2.6 0.1 copy-done.3
  2.7 0.6 pad.16.weights
  3.3 1.0 reshape.120
  4.3 0.0 copy-start
  4.3 0.1 copy.11
  4.4 0.2 reshape.121
  4.6 0.7 copy-done
  5.3 0.9 pad_maximum_fusion.packed
  6.2 133.0 %shard_map.73 = f32[8,64,64]{2,1,0:T(8,128)} custom-call(s32[64]{0:T(128)} %bitcast.9, s32[64]{0:T(128)} %copy-done.4, s32[8,8]{1,0:T(8,128)} %couple_ref.1, f32[8,8]{1,0:T(8,128)} %scale_ref.1, f32[8,16]{1,0:T(8,128)} %rate_ref.1, f32[8,80,256]{2,1,0:T(8,128)} %pad_maximum_fusion.packed, f32[2,2,64,256]{3,2,1,0:T(8,128)} %shard.1, f32[8,128]{1,0:T(8,128)} %pad.16.weights, ...), custom_call_target="tpu_custom_call" | custom-call | tf_op jit(solution)/shard_map/pallas_call | solution.py:504
  139.2 1.7 %reshape.123 = f32[8,4096]{1,0:T(8,128)} reshape(f32[8,64,64]{2,1,0:T(8,128)} %shard_map.73) | data formatting | bytes 262144 | tf_op jit(solution)/shard_map/reshape | solution.py:531
  (4 shorter events, 0.0 us)
Async XLA Ops:
  0.0 0.7 copy-start.1
  0.8 0.5 copy-start.4
  1.3 0.7 copy-start.2
  2.0 0.7 copy-start.3
  4.3 1.0 copy-start
